TPU v7x, 32 devices: a whole 2x2x4 slice. The times are simulated.
32 devices in a mesh: die: 4 (over y, x), tile: 8 (over z, core).
Axes of the slice: x: 2, y: 2, z: 4, core: 2. Of those that a mesh axis runs over, the one named last changes fastest.
Arguments:
- source_heating: float32 [16, 128, 2048], P('die', 'tile'), may hold values from -96 to 96, as said below
- material_thermal_values: float32 [6], replicated, may hold values from 0.5 to 8
- layer_material: int32 [16], P('die'), may hold values from 0 to 5
- via_conductance: float32 [4], P('die'), may hold values from 2 to 16
- via_blocks: int32 [4, 24, 4], P('die'), may hold values from 0 to 2048, as said below
Outputs:
- thermal_solution: float32 [16, 128, 2048], P('die', 'tile')
- balance_defect: float32 [16, 128, 2048], P('die', 'tile')
Inputs may be any that keep to these rules, and one draw needn't show every extreme that they name: `via_blocks`: entry (d, b) is (first row, first column, height, width) of via block b on top of die d, joining die d's top layer to die d + 1's bottom layer, or to the cooled lid for the top die. Height is 8, 16 or 32 and width 16, 32 or 64, each cut to the plane's 128 x 2048 cells; every block lies inside the plane; blocks may intersect. `source_heating`: heat per cell.
All inputs are finite; a program needn't handle non-finite values.
Results may differ from a plain program's by a relative error of at most 0.0003.
Values sent between devices are 32-bit elements; how exact they have to be, the bound alone decides.
No kernel may reach another device: no remote copies, remote signals or barrier semaphores. Data moves between devices by JAX's collectives and lax.ppermute only.
A program may use at most 128 MiB of HBM per device.

v0:
```python
import jax
import jax.numpy as jnp
from jax import lax
from jax.sharding import PartitionSpec as P

NU = 2
NC = 6


OMEGA = 0.8


def from_behind(value, axis, steps):
    count = lax.axis_size(axis)
    leading, last = (max(0, -steps), min(count, count - steps))
    return lax.ppermute(value, axis, [(source, source + steps) for source in range(leading, last)])


def padded_2(x, sides, width):
    for axis, dim in sides:
        size, length = (lax.axis_size(axis), x.shape[dim])
        up = [(i, (i + 1) % size) for i in range(size - 1)]
        down = [(j, i) for i, j in up]
        last = lax.slice_in_dim(x, length - width, length, axis=dim)
        leading = lax.slice_in_dim(x, 0, width, axis=dim)
        before = lax.ppermute(last, axis, up)
        after = lax.ppermute(leading, axis, down)
        x = jnp.concatenate([before, x, after], axis=dim)
    return x


def block_sums(field):
    depth, height, lateral_extent = field.shape
    return field.reshape(depth, height // 4, 4, lateral_extent // 4, 4).sum(axis=(2, 4))


def spread_out(field):
    return jnp.repeat(jnp.repeat(field, 4, axis=1), 4, axis=2)


def stencil(padded, field, stencil_coefficients, diagonal, upper, lower):
    side = (
        padded[1:-1, 2:, 1:-1]
        + padded[1:-1, :-2, 1:-1]
        + padded[1:-1, 1:-1, 2:]
        + padded[1:-1, 1:-1, :-2]
    )
    return (
        diagonal * field
        - stencil_coefficients[:, None, None] * side
        - upper * padded[2:, 1:-1, 1:-1]
        - lower * padded[:-2, 1:-1, 1:-1]
    )


def local(source_heating, material_thermal_values, layer_material, via_conductance, via_blocks):
    layer_list, rows, width = source_heating.shape
    tile_pos = lax.axis_index("tile")
    onehot = (
        layer_material[:, None]
        == jnp.arange(material_thermal_values.shape[0], dtype=jnp.int32)[None, :]
    ).astype(jnp.float32)
    layer_cond = jnp.sum(onehot * material_thermal_values[None, :], axis=1)
    following = jnp.concatenate([layer_cond[1:], layer_cond[-1:]])
    vertical = 2.0 * layer_cond * following / (layer_cond + following)
    row_ids = tile_pos * rows + jnp.arange(rows, dtype=jnp.int32)
    col_ids = jnp.arange(width, dtype=jnp.int32)
    blocks = via_blocks[0]
    input_rows = (
        (row_ids[None, :] >= blocks[:, 0:1]) & (row_ids[None, :] < blocks[:, 0:1] + blocks[:, 2:3])
    ).astype(jnp.float32)
    in_cols = (
        (col_ids[None, :] >= blocks[:, 1:2]) & (col_ids[None, :] < blocks[:, 1:2] + blocks[:, 3:4])
    ).astype(jnp.float32)
    via_plane = (
        jnp.dot(
            input_rows.T,
            in_cols,
            precision=lax.Precision.HIGHEST,
            preferred_element_type=jnp.float32,
        )
        * via_conductance[0]
    )
    placed_above = jnp.arange(layer_list, dtype=jnp.int32) == layer_list - 1
    upper_zero = jnp.where(placed_above[:, None, None], via_plane[None], vertical[:, None, None])
    below = from_behind(via_plane, "die", 1)
    lower_zero = jnp.concatenate([below[None], upper_zero[:-1]], axis=0)
    upper_one = block_sums(upper_zero)
    lower_one = block_sums(lower_zero)
    uppers = [upper_zero, upper_one, block_sums(upper_one)]
    lowers = [lower_zero, lower_one, block_sums(lower_one)]
    stencil_coefficients = [layer_cond, layer_cond * 4.0, layer_cond * 16.0]
    diagonals = [
        4.0 * stencil_coefficients[lev][:, None, None] + uppers[lev] + lowers[lev]
        for lev in range(3)
    ]

    def conduction_product(field, level):
        if level == 0:
            padded = padded_2(field, (("die", 0), ("tile", 1)), 1)
        elif level == 1:
            padded = padded_2(field, (("die", 0), ("tile", 1)), 1)
        else:
            padded = padded_2(field, (("die", 0), ("tile", 1)), 1)
        padded = jnp.pad(padded, ((0, 0), (0, 0), (1, 1)))
        return stencil(
            padded,
            field,
            stencil_coefficients[level],
            diagonals[level],
            uppers[level],
            lowers[level],
        )

    def coarse_solve(rhs):
        field = OMEGA * rhs / diagonals[2]
        for sweep_index in range(NC - 1):
            field = field + OMEGA * (rhs - conduction_product(field, 2)) / diagonals[2]
        return field

    def smooth(field, rhs, level):
        return field + OMEGA * (rhs - conduction_product(field, level)) / diagonals[level]

    def hierarchy_round(level, rhs, field):
        if level == 2:
            return coarse_solve(rhs)
        sweeps = NU
        if field is None:
            field = OMEGA * rhs / diagonals[level]
            sweeps = sweeps - 1
        for sweep_index in range(sweeps):
            field = smooth(field, rhs, level)
        remainder = rhs - conduction_product(field, level)
        field = field + spread_out(hierarchy_round(level + 1, block_sums(remainder), None))
        for sweep_index in range(NU):
            field = smooth(field, rhs, level)
        return field

    thermal_solution = hierarchy_round(0, source_heating, None)
    thermal_solution = hierarchy_round(0, source_heating, thermal_solution)
    balance_defect = source_heating - conduction_product(thermal_solution, 0)
    return (thermal_solution, balance_defect)


def solution(mesh):
    in_specs = (P("die", "tile", None), P(), P("die"), P("die"), P("die", None, None))
    out_specs = (P("die", "tile", None), P("die", "tile", None))
    return jax.shard_map(local, mesh=mesh, in_specs=in_specs, out_specs=out_specs, check_vma=False)
```

profile of v0, /device:TPU:1, one launch (start us, length us, event | category | flops | bytes accessed | tf_op | source)
XLA Modules:
  0.0 586.8 jit_solution(6602612465182000873)
XLA Ops:
  2.4 3.9 collective-permute-start
  8.7 5.7 broadcast_in_dim.59
  14.4 14.3 %concatenate.479 = f32[3,4,4,512,4]{4,3,2,1,0:T(8,128)} reshape(f32[3,16,2048]{2,1,0:T(8,128)S(1)} %slice.1350) | data formatting | bytes 786432 | tf_op jit(solution)/shard_map/concatenate | solution.py:87
  36.6 5.7 concatenate.478
  48.6 4.6 constant_dynamic-update-slice_fusion.1
  54.5 4.3 collective-permute-start.5
  60.1 10.6 %constant_dynamic-update-slice_fusion = f32[4,4,4,512,4]{4,3,2,1,0:T(8,128)} fusion(f32[4,4,4,512,4]{4,3,2,1,0:T(8,128)} %constant_dynamic-update-slice_fusion.1, f32[3,4,4,512,4]{4,3,2,1,0:T(8,128)} %concatenate.479), kind=kLoop, calls=%fused_computation.569 | loop fusion | bytes 25165824 | tf_op jit(solution)/shard_map/concatenate | solution.py:87
  72.7 3.8 collective-permute-start.8
  76.5 8.2 %fusion.281 = (f32[4,512]{1,0:T(4,128)S(1)}, f32[4,4,512]{2,1,0:T(4,128)S(1)}) fusion(f32[4,4,4,512,4]{4,3,2,1,0:T(8,128)} %constant_dynamic-update-slice_fusion), kind=kLoop, calls=%fused_computation.745 | loop fusion | flops 251904 | bytes 565248 | tf_op jit(solution)/shard_map/reduce_sum | solution.py:34
  85.9 18.7 %reshape.283 = f32[4,4,4,512,4]{4,3,2,1,0:T(8,128)} reshape(f32[4,16,2048]{2,1,0:T(8,128)S(1)} %fusion.10) | data formatting | bytes 1048576 | tf_op jit(solution)/shard_map/reshape | solution.py:34
  104.5 7.0 %reduce_sum.97 = f32[4,4,512]{2,1,0:T(4,128)S(1)} reduce(f32[4,4,4,512,4]{4,3,2,1,0:T(8,128)} %reshape.283, f32[]{:T(128)} %constant.10.clone.1), dimensions={2,4}, to_apply=%region_1.2 | reduce | flops 122880 | bytes 557060 | tf_op jit(solution)/shard_map/reduce_sum | solution.py:34
  111.6 4.6 collective-permute-start.9
  117.6 4.0 collective-permute-done.10
  128.3 4.3 collective-permute-start.13
  139.3 5.2 collective-permute-start.16
  147.5 4.0 collective-permute-start.17
  154.1 5.3 collective-permute-start.20
  161.6 4.5 collective-permute-start.21
  168.8 5.0 collective-permute-start.24
  176.0 5.2 collective-permute-start.25
  183.8 5.0 collective-permute-start.28
  191.1 5.4 collective-permute-start.29
  199.2 5.0 collective-permute-start.32
  206.4 5.4 collective-permute-start.33
  214.5 5.0 collective-permute-start.36
  220.8 4.8 collective-permute-start.37
  226.9 4.5 collective-permute-done.38
  233.4 5.3 collective-permute-start.40
  239.9 4.5 collective-permute-start.41
  250.8 5.8 collective-permute-start.44
  268.2 3.8 collective-permute-done.46
  274.0 5.6 collective-permute-start.48
  286.5 3.8 collective-permute-done.50
  292.3 5.7 collective-permute-start.52
  304.8 3.8 collective-permute-done.54
  310.7 5.7 collective-permute-start.56
  323.2 3.8 collective-permute-done.58
  329.0 5.7 collective-permute-start.60
  341.5 3.8 collective-permute-done.62
  347.3 5.7 collective-permute-start.64
  355.3 18.7 %reshape.286 = f32[4,4,4,512,4]{4,3,2,1,0:T(8,128)} reshape(f32[4,16,2048]{2,1,0:T(8,128)S(1)} %fusion.37) | data formatting | bytes 1048576 | tf_op jit(solution)/shard_map/reshape | solution.py:34
  374.0 7.0 %reduce_sum.133 = f32[4,4,512]{2,1,0:T(4,128)S(1)} reduce(f32[4,4,4,512,4]{4,3,2,1,0:T(8,128)} %reshape.286, f32[]{:T(128)} %constant.10.clone.1), dimensions={2,4}, to_apply=%region_10.11 | reduce | flops 122880 | bytes 557060 | tf_op jit(solution)/shard_map/reduce_sum | solution.py:34
  390.2 5.7 collective-permute-start.68
  405.9 5.6 collective-permute-start.72
  414.4 4.0 collective-permute-start.73
  421.1 5.3 collective-permute-start.76
  428.6 4.5 collective-permute-start.77
  435.8 5.0 collective-permute-start.80
  443.0 5.2 collective-permute-start.81
  450.8 5.0 collective-permute-start.84
  458.1 5.4 collective-permute-start.85
  466.2 5.0 collective-permute-start.88
  473.4 5.4 collective-permute-start.89
  481.5 5.0 collective-permute-start.92
  487.8 4.8 collective-permute-start.93
  493.9 4.5 collective-permute-done.94
  500.4 5.3 collective-permute-start.96
  506.8 4.5 collective-permute-start.97
  517.7 5.6 collective-permute-start.100
  535.2 3.8 collective-permute-done.102
  541.0 5.6 collective-permute-start.104
  553.5 3.8 collective-permute-done.106
  559.3 5.7 collective-permute-start.108
  577.6 5.7 collective-permute-start.112
  (341 shorter events, 219.4 us)
Async XLA Ops:
  2.4 29.2 %collective-permute-start = (f32[16,2048]{1,0:T(8,128)S(1)}, f32[16,2048]{1,0:T(8,128)S(1)}, u32[]{:S(2)}, u32[]{:S(2)}) collective-permute-start(f32[16,2048]{1,0:T(8,128)S(1)} %convolution_multiply_fusion), channel_id=1, source_target_pairs={{0,8},{8,16},{16,24},{1,9},{9,17},{17,25},{2,10},{10,18},{18,26},{... | collective-permute-start | bytes 393224 | tf_op jit(solution)/shard_map/ppermute | solution.py:16
  31.9 10.4 %collective-permute-start.1 = (f32[1,16,2048]{2,1,0:T(8,128)S(1)}, f32[1,16,2048]{2,1,0:T(8,128)S(1)}, u32[]{:S(2)}, u32[]{:S(2)}) collective-permute-start(f32[1,16,2048]{2,1,0:T(8,128)S(1)} %get-tuple-element.55), channel_id=1, source_target_pairs={{0,8},{8,16},{16,24},{1,9},{9,17},{17,25},{2,10},{10,18},{18,26},{... | collective-permute-start | bytes 393224 | tf_op jit(solution)/shard_map/ppermute | solution.py:26
  35.0 7.3 %collective-permute-start.2 = (f32[1,16,2048]{2,1,0:T(8,128)S(1)}, f32[1,16,2048]{2,1,0:T(8,128)S(1)}, u32[]{:S(2)}, u32[]{:S(2)}) collective-permute-start(f32[1,16,2048]{2,1,0:T(8,128)S(1)} %get-tuple-element.54), channel_id=1, source_target_pairs={{8,0},{16,8},{24,16},{9,1},{17,9},{25,17},{10,2},{18,10},{26,18},{... | collective-permute-start | bytes 393224 | tf_op jit(solution)/shard_map/ppermute | solution.py:27
  42.4 10.9 %collective-permute-start.3 = (f32[6,1,2048]{2,1,0:T(1,128)S(1)}, f32[6,1,2048]{2,1,0:T(1,128)S(1)}, u32[]{:S(2)}, u32[]{:S(2)}) collective-permute-start(f32[6,1,2048]{2,1,0:T(1,128)S(1)} %get-tuple-element.35), channel_id=1, source_target_pairs={{1,0},{2,1},{3,2},{4,3},{5,4},{6,5},{7,6},{9,8},{10,9},{11,10},{12... | collective-permute-start | bytes 147464 | tf_op jit(solution)/shard_map/ppermute | solution.py:27
  45.5 7.8 %collective-permute-start.4 = (f32[6,1,2048]{2,1,0:T(1,128)S(1)}, f32[6,1,2048]{2,1,0:T(1,128)S(1)}, u32[]{:S(2)}, u32[]{:S(2)}) collective-permute-start(f32[6,1,2048]{2,1,0:T(1,128)S(1)} %get-tuple-element.34), channel_id=1, source_target_pairs={{0,1},{1,2},{2,3},{3,4},{4,5},{5,6},{6,7},{8,9},{9,10},{10,11},{11... | collective-permute-start | bytes 147464 | tf_op jit(solution)/shard_map/ppermute | solution.py:26
  54.5 16.2 %collective-permute-start.5 = (f32[1,16,2048]{2,1,0:T(8,128)S(1)}, f32[1,16,2048]{2,1,0:T(8,128)S(1)}, u32[]{:S(2)}, u32[]{:S(2)}) collective-permute-start(f32[1,16,2048]{2,1,0:T(8,128)S(1)} %get-tuple-element.53), channel_id=1, source_target_pairs={{0,8},{8,16},{16,24},{1,9},{9,17},{17,25},{2,10},{10,18},{18,26},{... | collective-permute-start | bytes 393224 | tf_op jit(solution)/shard_map/ppermute | solution.py:26
  58.8 11.9 %collective-permute-start.6 = (f32[1,16,2048]{2,1,0:T(8,128)S(1)}, f32[1,16,2048]{2,1,0:T(8,128)S(1)}, u32[]{:S(2)}, u32[]{:S(2)}) collective-permute-start(f32[1,16,2048]{2,1,0:T(8,128)S(1)} %get-tuple-element.52), channel_id=1, source_target_pairs={{8,0},{16,8},{24,16},{9,1},{17,9},{25,17},{10,2},{18,10},{26,18},{... | collective-permute-start | bytes 393224 | tf_op jit(solution)/shard_map/ppermute | solution.py:27
  70.8 14.0 %collective-permute-start.7 = (f32[6,1,2048]{2,1,0:T(1,128)S(1)}, f32[6,1,2048]{2,1,0:T(1,128)S(1)}, u32[]{:S(2)}, u32[]{:S(2)}) collective-permute-start(f32[6,1,2048]{2,1,0:T(1,128)S(1)} %get-tuple-element.33), channel_id=1, source_target_pairs={{1,0},{2,1},{3,2},{4,3},{5,4},{6,5},{7,6},{9,8},{10,9},{11,10},{12... | collective-permute-start | bytes 147464 | tf_op jit(solution)/shard_map/ppermute | solution.py:27
  72.7 12.0 %collective-permute-start.8 = (f32[6,1,2048]{2,1,0:T(1,128)S(1)}, f32[6,1,2048]{2,1,0:T(1,128)S(1)}, u32[]{:S(2)}, u32[]{:S(2)}) collective-permute-start(f32[6,1,2048]{2,1,0:T(1,128)S(1)} %get-tuple-element.32), channel_id=1, source_target_pairs={{0,1},{1,2},{2,3},{3,4},{4,5},{5,6},{6,7},{8,9},{9,10},{10,11},{11... | collective-permute-start | bytes 147464 | tf_op jit(solution)/shard_map/ppermute | solution.py:26
  111.6 5.9 %collective-permute-start.9 = (f32[1,4,512]{2,1,0:T(4,128)S(1)}, f32[1,4,512]{2,1,0:T(4,128)S(1)}, u32[]{:S(2)}, u32[]{:S(2)}) collective-permute-start(f32[1,4,512]{2,1,0:T(4,128)S(1)} %get-tuple-element.87), channel_id=1, source_target_pairs={{0,8},{8,16},{16,24},{1,9},{9,17},{17,25},{2,10},{10,18},{18,26},{... | collective-permute-start | bytes 24584 | tf_op jit(solution)/shard_map/ppermute | solution.py:26
  137.0 8.4 %collective-permute-start.15 = (f32[6,1,512]{2,1,0:T(1,128)S(1)}, f32[6,1,512]{2,1,0:T(1,128)S(1)}, u32[]{:S(2)}, u32[]{:S(2)}) collective-permute-start(f32[6,1,512]{2,1,0:T(1,128)S(1)} %get-tuple-element.69), channel_id=1, source_target_pairs={{1,0},{2,1},{3,2},{4,3},{5,4},{6,5},{7,6},{9,8},{10,9},{11,10},{12... | collective-permute-start | bytes 36872 | tf_op jit(solution)/shard_map/ppermute | solution.py:27
  139.3 6.1 %collective-permute-start.16 = (f32[6,1,512]{2,1,0:T(1,128)S(1)}, f32[6,1,512]{2,1,0:T(1,128)S(1)}, u32[]{:S(2)}, u32[]{:S(2)}) collective-permute-start(f32[6,1,512]{2,1,0:T(1,128)S(1)} %get-tuple-element.68), channel_id=1, source_target_pairs={{0,1},{1,2},{2,3},{3,4},{4,5},{5,6},{6,7},{8,9},{9,10},{10,11},{11... | collective-permute-start | bytes 36872 | tf_op jit(solution)/shard_map/ppermute | solution.py:26
  152.2 7.2 %collective-permute-start.19 = (f32[6,1,128]{2,0,1:T(8,128)S(1)}, f32[6,1,128]{2,0,1:T(8,128)S(1)}, u32[]{:S(2)}, u32[]{:S(2)}) collective-permute-start(f32[6,1,128]{2,0,1:T(8,128)S(1)} %pad_maximum_fusion.199), channel_id=1, source_target_pairs={{1,0},{2,1},{3,2},{4,3},{5,4},{6,5},{7,6},{9,8},{10,9},{11,10},{12... | collective-permute-start | bytes 9224 | tf_op jit(solution)/shard_map/ppermute | solution.py:27
  154.1 6.0 %collective-permute-start.20 = (f32[6,1,128]{2,0,1:T(8,128)S(1)}, f32[6,1,128]{2,0,1:T(8,128)S(1)}, u32[]{:S(2)}, u32[]{:S(2)}) collective-permute-start(f32[6,1,128]{2,0,1:T(8,128)S(1)} %pad_maximum_fusion.199), channel_id=1, source_target_pairs={{0,1},{1,2},{2,3},{3,4},{4,5},{5,6},{6,7},{8,9},{9,10},{10,11},{11... | collective-permute-start | bytes 9224 | tf_op jit(solution)/shard_map/ppermute | solution.py:26
  166.9 7.0 %collective-permute-start.23 = (f32[6,1,128]{2,0,1:T(8,128)S(1)}, f32[6,1,128]{2,0,1:T(8,128)S(1)}, u32[]{:S(2)}, u32[]{:S(2)}) collective-permute-start(f32[6,1,128]{2,0,1:T(8,128)S(1)} %pad_maximum_fusion.202), channel_id=1, source_target_pairs={{1,0},{2,1},{3,2},{4,3},{5,4},{6,5},{7,6},{9,8},{10,9},{11,10},{12... | collective-permute-start | bytes 9224 | tf_op jit(solution)/shard_map/ppermute | solution.py:27
  174.7 6.5 %collective-permute-start.26 = (f32[1,1,128]{2,0,1:T(1,128)S(1)}, f32[1,1,128]{2,0,1:T(1,128)S(1)}, u32[]{:S(2)}, u32[]{:S(2)}) collective-permute-start(f32[1,1,128]{2,0,1:T(1,128)S(1)} %get-tuple-element.118), channel_id=1, source_target_pairs={{8,0},{16,8},{24,16},{9,1},{17,9},{25,17},{10,2},{18,10},{26,18},{... | collective-permute-start | bytes 1544 | tf_op jit(solution)/shard_map/ppermute | solution.py:27
  181.9 7.0 %collective-permute-start.27 = (f32[6,1,128]{2,0,1:T(8,128)S(1)}, f32[6,1,128]{2,0,1:T(8,128)S(1)}, u32[]{:S(2)}, u32[]{:S(2)}) collective-permute-start(f32[6,1,128]{2,0,1:T(8,128)S(1)} %pad_maximum_fusion.205), channel_id=1, source_target_pairs={{1,0},{2,1},{3,2},{4,3},{5,4},{6,5},{7,6},{9,8},{10,9},{11,10},{12... | collective-permute-start | bytes 9224 | tf_op jit(solution)/shard_map/ppermute | solution.py:27
  189.8 6.7 %collective-permute-start.30 = (f32[1,1,128]{2,0,1:T(1,128)S(1)}, f32[1,1,128]{2,0,1:T(1,128)S(1)}, u32[]{:S(2)}, u32[]{:S(2)}) collective-permute-start(f32[1,1,128]{2,0,1:T(1,128)S(1)} %get-tuple-element.114), channel_id=1, source_target_pairs={{8,0},{16,8},{24,16},{9,1},{17,9},{25,17},{10,2},{18,10},{26,18},{... | collective-permute-start | bytes 1544 | tf_op jit(solution)/shard_map/ppermute | solution.py:27
  191.1 6.1 %collective-permute-start.29 = (f32[1,1,128]{2,0,1:T(1,128)S(1)}, f32[1,1,128]{2,0,1:T(1,128)S(1)}, u32[]{:S(2)}, u32[]{:S(2)}) collective-permute-start(f32[1,1,128]{2,0,1:T(1,128)S(1)} %get-tuple-element.115), channel_id=1, source_target_pairs={{0,8},{8,16},{16,24},{1,9},{9,17},{17,25},{2,10},{10,18},{18,26},{... | collective-permute-start | bytes 1544 | tf_op jit(solution)/shard_map/ppermute | solution.py:26
  197.3 7.0 %collective-permute-start.31 = (f32[6,1,128]{2,0,1:T(8,128)S(1)}, f32[6,1,128]{2,0,1:T(8,128)S(1)}, u32[]{:S(2)}, u32[]{:S(2)}) collective-permute-start(f32[6,1,128]{2,0,1:T(8,128)S(1)} %pad_maximum_fusion.208), channel_id=1, source_target_pairs={{1,0},{2,1},{3,2},{4,3},{5,4},{6,5},{7,6},{9,8},{10,9},{11,10},{12... | collective-permute-start | bytes 9224 | tf_op jit(solution)/shard_map/ppermute | solution.py:27
  205.1 6.7 %collective-permute-start.34 = (f32[1,1,128]{2,0,1:T(1,128)S(1)}, f32[1,1,128]{2,0,1:T(1,128)S(1)}, u32[]{:S(2)}, u32[]{:S(2)}) collective-permute-start(f32[1,1,128]{2,0,1:T(1,128)S(1)} %get-tuple-element.110), channel_id=1, source_target_pairs={{8,0},{16,8},{24,16},{9,1},{17,9},{25,17},{10,2},{18,10},{26,18},{... | collective-permute-start | bytes 1544 | tf_op jit(solution)/shard_map/ppermute | solution.py:27
  206.4 6.1 %collective-permute-start.33 = (f32[1,1,128]{2,0,1:T(1,128)S(1)}, f32[1,1,128]{2,0,1:T(1,128)S(1)}, u32[]{:S(2)}, u32[]{:S(2)}) collective-permute-start(f32[1,1,128]{2,0,1:T(1,128)S(1)} %get-tuple-element.111), channel_id=1, source_target_pairs={{0,8},{8,16},{16,24},{1,9},{9,17},{17,25},{2,10},{10,18},{18,26},{... | collective-permute-start | bytes 1544 | tf_op jit(solution)/shard_map/ppermute | solution.py:26
  212.6 7.0 %collective-permute-start.35 = (f32[6,1,128]{2,0,1:T(8,128)S(1)}, f32[6,1,128]{2,0,1:T(8,128)S(1)}, u32[]{:S(2)}, u32[]{:S(2)}) collective-permute-start(f32[6,1,128]{2,0,1:T(8,128)S(1)} %pad_maximum_fusion.211), channel_id=1, source_target_pairs={{1,0},{2,1},{3,2},{4,3},{5,4},{6,5},{7,6},{9,8},{10,9},{11,10},{12... | collective-permute-start | bytes 9224 | tf_op jit(solution)/shard_map/ppermute | solution.py:27
  220.8 6.1 %collective-permute-start.37 = (f32[1,4,512]{2,1,0:T(4,128)S(1)}, f32[1,4,512]{2,1,0:T(4,128)S(1)}, u32[]{:S(2)}, u32[]{:S(2)}) collective-permute-start(f32[1,4,512]{2,1,0:T(4,128)S(1)} %get-tuple-element.83), channel_id=1, source_target_pairs={{0,8},{8,16},{16,24},{1,9},{9,17},{17,25},{2,10},{10,18},{18,26},{... | collective-permute-start | bytes 24584 | tf_op jit(solution)/shard_map/ppermute | solution.py:26
  231.5 7.3 %collective-permute-start.39 = (f32[6,1,512]{2,1,0:T(1,128)S(1)}, f32[6,1,512]{2,1,0:T(1,128)S(1)}, u32[]{:S(2)}, u32[]{:S(2)}) collective-permute-start(f32[6,1,512]{2,1,0:T(1,128)S(1)} %get-tuple-element.67), channel_id=1, source_target_pairs={{1,0},{2,1},{3,2},{4,3},{5,4},{6,5},{7,6},{9,8},{10,9},{11,10},{12... | collective-permute-start | bytes 36872 | tf_op jit(solution)/shard_map/ppermute | solution.py:27
  233.4 6.2 %collective-permute-start.40 = (f32[6,1,512]{2,1,0:T(1,128)S(1)}, f32[6,1,512]{2,1,0:T(1,128)S(1)}, u32[]{:S(2)}, u32[]{:S(2)}) collective-permute-start(f32[6,1,512]{2,1,0:T(1,128)S(1)} %get-tuple-element.66), channel_id=1, source_target_pairs={{0,1},{1,2},{2,3},{3,4},{4,5},{5,6},{6,7},{8,9},{9,10},{10,11},{11... | collective-permute-start | bytes 36872 | tf_op jit(solution)/shard_map/ppermute | solution.py:26
  248.8 7.8 %collective-permute-start.43 = (f32[6,1,512]{2,1,0:T(1,128)S(1)}, f32[6,1,512]{2,1,0:T(1,128)S(1)}, u32[]{:S(2)}, u32[]{:S(2)}) collective-permute-start(f32[6,1,512]{2,1,0:T(1,128)S(1)} %get-tuple-element.65), channel_id=1, source_target_pairs={{1,0},{2,1},{3,2},{4,3},{5,4},{6,5},{7,6},{9,8},{10,9},{11,10},{12... | collective-permute-start | bytes 36872 | tf_op jit(solution)/shard_map/ppermute | solution.py:27
  250.8 6.4 %collective-permute-start.44 = (f32[6,1,512]{2,1,0:T(1,128)S(1)}, f32[6,1,512]{2,1,0:T(1,128)S(1)}, u32[]{:S(2)}, u32[]{:S(2)}) collective-permute-start(f32[6,1,512]{2,1,0:T(1,128)S(1)} %get-tuple-element.64), channel_id=1, source_target_pairs={{0,1},{1,2},{2,3},{3,4},{4,5},{5,6},{6,7},{8,9},{9,10},{10,11},{11... | collective-permute-start | bytes 36872 | tf_op jit(solution)/shard_map/ppermute | solution.py:26
  272.1 7.6 %collective-permute-start.47 = (f32[6,1,2048]{2,1,0:T(1,128)S(1)}, f32[6,1,2048]{2,1,0:T(1,128)S(1)}, u32[]{:S(2)}, u32[]{:S(2)}) collective-permute-start(f32[6,1,2048]{2,1,0:T(1,128)S(1)} %get-tuple-element.31), channel_id=1, source_target_pairs={{1,0},{2,1},{3,2},{4,3},{5,4},{6,5},{7,6},{9,8},{10,9},{11,10},{12... | collective-permute-start | bytes 147464 | tf_op jit(solution)/shard_map/ppermute | solution.py:27
  274.0 6.8 %collective-permute-start.48 = (f32[6,1,2048]{2,1,0:T(1,128)S(1)}, f32[6,1,2048]{2,1,0:T(1,128)S(1)}, u32[]{:S(2)}, u32[]{:S(2)}) collective-permute-start(f32[6,1,2048]{2,1,0:T(1,128)S(1)} %get-tuple-element.30), channel_id=1, source_target_pairs={{0,1},{1,2},{2,3},{3,4},{4,5},{5,6},{6,7},{8,9},{9,10},{10,11},{11... | collective-permute-start | bytes 147464 | tf_op jit(solution)/shard_map/ppermute | solution.py:26
  290.4 7.6 %collective-permute-start.51 = (f32[6,1,2048]{2,1,0:T(1,128)S(1)}, f32[6,1,2048]{2,1,0:T(1,128)S(1)}, u32[]{:S(2)}, u32[]{:S(2)}) collective-permute-start(f32[6,1,2048]{2,1,0:T(1,128)S(1)} %get-tuple-element.29), channel_id=1, source_target_pairs={{1,0},{2,1},{3,2},{4,3},{5,4},{6,5},{7,6},{9,8},{10,9},{11,10},{12... | collective-permute-start | bytes 147464 | tf_op jit(solution)/shard_map/ppermute | solution.py:27
  292.3 6.8 %collective-permute-start.52 = (f32[6,1,2048]{2,1,0:T(1,128)S(1)}, f32[6,1,2048]{2,1,0:T(1,128)S(1)}, u32[]{:S(2)}, u32[]{:S(2)}) collective-permute-start(f32[6,1,2048]{2,1,0:T(1,128)S(1)} %get-tuple-element.28), channel_id=1, source_target_pairs={{0,1},{1,2},{2,3},{3,4},{4,5},{5,6},{6,7},{8,9},{9,10},{10,11},{11... | collective-permute-start | bytes 147464 | tf_op jit(solution)/shard_map/ppermute | solution.py:26
  308.7 7.6 %collective-permute-start.55 = (f32[6,1,2048]{2,1,0:T(1,128)S(1)}, f32[6,1,2048]{2,1,0:T(1,128)S(1)}, u32[]{:S(2)}, u32[]{:S(2)}) collective-permute-start(f32[6,1,2048]{2,1,0:T(1,128)S(1)} %get-tuple-element.27), channel_id=1, source_target_pairs={{1,0},{2,1},{3,2},{4,3},{5,4},{6,5},{7,6},{9,8},{10,9},{11,10},{12... | collective-permute-start | bytes 147464 | tf_op jit(solution)/shard_map/ppermute | solution.py:27
  310.7 6.8 %collective-permute-start.56 = (f32[6,1,2048]{2,1,0:T(1,128)S(1)}, f32[6,1,2048]{2,1,0:T(1,128)S(1)}, u32[]{:S(2)}, u32[]{:S(2)}) collective-permute-start(f32[6,1,2048]{2,1,0:T(1,128)S(1)} %get-tuple-element.26), channel_id=1, source_target_pairs={{0,1},{1,2},{2,3},{3,4},{4,5},{5,6},{6,7},{8,9},{9,10},{10,11},{11... | collective-permute-start | bytes 147464 | tf_op jit(solution)/shard_map/ppermute | solution.py:26
  327.1 7.6 %collective-permute-start.59 = (f32[6,1,2048]{2,1,0:T(1,128)S(1)}, f32[6,1,2048]{2,1,0:T(1,128)S(1)}, u32[]{:S(2)}, u32[]{:S(2)}) collective-permute-start(f32[6,1,2048]{2,1,0:T(1,128)S(1)} %get-tuple-element.25), channel_id=1, source_target_pairs={{1,0},{2,1},{3,2},{4,3},{5,4},{6,5},{7,6},{9,8},{10,9},{11,10},{12... | collective-permute-start | bytes 147464 | tf_op jit(solution)/shard_map/ppermute | solution.py:27
  329.0 6.8 %collective-permute-start.60 = (f32[6,1,2048]{2,1,0:T(1,128)S(1)}, f32[6,1,2048]{2,1,0:T(1,128)S(1)}, u32[]{:S(2)}, u32[]{:S(2)}) collective-permute-start(f32[6,1,2048]{2,1,0:T(1,128)S(1)} %get-tuple-element.24), channel_id=1, source_target_pairs={{0,1},{1,2},{2,3},{3,4},{4,5},{5,6},{6,7},{8,9},{9,10},{10,11},{11... | collective-permute-start | bytes 147464 | tf_op jit(solution)/shard_map/ppermute | solution.py:26
  345.4 7.6 %collective-permute-start.63 = (f32[6,1,2048]{2,1,0:T(1,128)S(1)}, f32[6,1,2048]{2,1,0:T(1,128)S(1)}, u32[]{:S(2)}, u32[]{:S(2)}) collective-permute-start(f32[6,1,2048]{2,1,0:T(1,128)S(1)} %get-tuple-element.23), channel_id=1, source_target_pairs={{1,0},{2,1},{3,2},{4,3},{5,4},{6,5},{7,6},{9,8},{10,9},{11,10},{12... | collective-permute-start | bytes 147464 | tf_op jit(solution)/shard_map/ppermute | solution.py:27
  347.3 6.8 %collective-permute-start.64 = (f32[6,1,2048]{2,1,0:T(1,128)S(1)}, f32[6,1,2048]{2,1,0:T(1,128)S(1)}, u32[]{:S(2)}, u32[]{:S(2)}) collective-permute-start(f32[6,1,2048]{2,1,0:T(1,128)S(1)} %get-tuple-element.22), channel_id=1, source_target_pairs={{0,1},{1,2},{2,3},{3,4},{4,5},{5,6},{6,7},{8,9},{9,10},{10,11},{11... | collective-permute-start | bytes 147464 | tf_op jit(solution)/shard_map/ppermute | solution.py:26
  388.0 7.9 %collective-permute-start.67 = (f32[6,1,512]{2,1,0:T(1,128)S(1)}, f32[6,1,512]{2,1,0:T(1,128)S(1)}, u32[]{:S(2)}, u32[]{:S(2)}) collective-permute-start(f32[6,1,512]{2,1,0:T(1,128)S(1)} %get-tuple-element.63), channel_id=1, source_target_pairs={{1,0},{2,1},{3,2},{4,3},{5,4},{6,5},{7,6},{9,8},{10,9},{11,10},{12... | collective-permute-start | bytes 36872 | tf_op jit(solution)/shard_map/ppermute | solution.py:27
  390.2 6.5 %collective-permute-start.68 = (f32[6,1,512]{2,1,0:T(1,128)S(1)}, f32[6,1,512]{2,1,0:T(1,128)S(1)}, u32[]{:S(2)}, u32[]{:S(2)}) collective-permute-start(f32[6,1,512]{2,1,0:T(1,128)S(1)} %get-tuple-element.62), channel_id=1, source_target_pairs={{0,1},{1,2},{2,3},{3,4},{4,5},{5,6},{6,7},{8,9},{9,10},{10,11},{11... | collective-permute-start | bytes 36872 | tf_op jit(solution)/shard_map/ppermute | solution.py:26
  403.9 7.6 %collective-permute-start.71 = (f32[6,1,512]{2,1,0:T(1,128)S(1)}, f32[6,1,512]{2,1,0:T(1,128)S(1)}, u32[]{:S(2)}, u32[]{:S(2)}) collective-permute-start(f32[6,1,512]{2,1,0:T(1,128)S(1)} %get-tuple-element.61), channel_id=1, source_target_pairs={{1,0},{2,1},{3,2},{4,3},{5,4},{6,5},{7,6},{9,8},{10,9},{11,10},{12... | collective-permute-start | bytes 36872 | tf_op jit(solution)/shard_map/ppermute | solution.py:27
  405.9 6.4 %collective-permute-start.72 = (f32[6,1,512]{2,1,0:T(1,128)S(1)}, f32[6,1,512]{2,1,0:T(1,128)S(1)}, u32[]{:S(2)}, u32[]{:S(2)}) collective-permute-start(f32[6,1,512]{2,1,0:T(1,128)S(1)} %get-tuple-element.60), channel_id=1, source_target_pairs={{0,1},{1,2},{2,3},{3,4},{4,5},{5,6},{6,7},{8,9},{9,10},{10,11},{11... | collective-permute-start | bytes 36872 | tf_op jit(solution)/shard_map/ppermute | solution.py:26
  419.1 7.3 %collective-permute-start.75 = (f32[6,1,128]{2,0,1:T(8,128)S(1)}, f32[6,1,128]{2,0,1:T(8,128)S(1)}, u32[]{:S(2)}, u32[]{:S(2)}) collective-permute-start(f32[6,1,128]{2,0,1:T(8,128)S(1)} %pad_maximum_fusion.214), channel_id=1, source_target_pairs={{1,0},{2,1},{3,2},{4,3},{5,4},{6,5},{7,6},{9,8},{10,9},{11,10},{12... | collective-permute-start | bytes 9224 | tf_op jit(solution)/shard_map/ppermute | solution.py:27
  421.1 6.1 %collective-permute-start.76 = (f32[6,1,128]{2,0,1:T(8,128)S(1)}, f32[6,1,128]{2,0,1:T(8,128)S(1)}, u32[]{:S(2)}, u32[]{:S(2)}) collective-permute-start(f32[6,1,128]{2,0,1:T(8,128)S(1)} %pad_maximum_fusion.214), channel_id=1, source_target_pairs={{0,1},{1,2},{2,3},{3,4},{4,5},{5,6},{6,7},{8,9},{9,10},{10,11},{11... | collective-permute-start | bytes 9224 | tf_op jit(solution)/shard_map/ppermute | solution.py:26
  433.9 7.0 %collective-permute-start.79 = (f32[6,1,128]{2,0,1:T(8,128)S(1)}, f32[6,1,128]{2,0,1:T(8,128)S(1)}, u32[]{:S(2)}, u32[]{:S(2)}) collective-permute-start(f32[6,1,128]{2,0,1:T(8,128)S(1)} %pad_maximum_fusion.217), channel_id=1, source_target_pairs={{1,0},{2,1},{3,2},{4,3},{5,4},{6,5},{7,6},{9,8},{10,9},{11,10},{12... | collective-permute-start | bytes 9224 | tf_op jit(solution)/shard_map/ppermute | solution.py:27
  441.7 6.5 %collective-permute-start.82 = (f32[1,1,128]{2,0,1:T(1,128)S(1)}, f32[1,1,128]{2,0,1:T(1,128)S(1)}, u32[]{:S(2)}, u32[]{:S(2)}) collective-permute-start(f32[1,1,128]{2,0,1:T(1,128)S(1)} %get-tuple-element.98), channel_id=1, source_target_pairs={{8,0},{16,8},{24,16},{9,1},{17,9},{25,17},{10,2},{18,10},{26,18},{... | collective-permute-start | bytes 1544 | tf_op jit(solution)/shard_map/ppermute | solution.py:27
  448.9 7.0 %collective-permute-start.83 = (f32[6,1,128]{2,0,1:T(8,128)S(1)}, f32[6,1,128]{2,0,1:T(8,128)S(1)}, u32[]{:S(2)}, u32[]{:S(2)}) collective-permute-start(f32[6,1,128]{2,0,1:T(8,128)S(1)} %pad_maximum_fusion.220), channel_id=1, source_target_pairs={{1,0},{2,1},{3,2},{4,3},{5,4},{6,5},{7,6},{9,8},{10,9},{11,10},{12... | collective-permute-start | bytes 9224 | tf_op jit(solution)/shard_map/ppermute | solution.py:27
  456.8 6.7 %collective-permute-start.86 = (f32[1,1,128]{2,0,1:T(1,128)S(1)}, f32[1,1,128]{2,0,1:T(1,128)S(1)}, u32[]{:S(2)}, u32[]{:S(2)}) collective-permute-start(f32[1,1,128]{2,0,1:T(1,128)S(1)} %get-tuple-element.94), channel_id=1, source_target_pairs={{8,0},{16,8},{24,16},{9,1},{17,9},{25,17},{10,2},{18,10},{26,18},{... | collective-permute-start | bytes 1544 | tf_op jit(solution)/shard_map/ppermute | solution.py:27
  458.1 6.1 %collective-permute-start.85 = (f32[1,1,128]{2,0,1:T(1,128)S(1)}, f32[1,1,128]{2,0,1:T(1,128)S(1)}, u32[]{:S(2)}, u32[]{:S(2)}) collective-permute-start(f32[1,1,128]{2,0,1:T(1,128)S(1)} %get-tuple-element.95), channel_id=1, source_target_pairs={{0,8},{8,16},{16,24},{1,9},{9,17},{17,25},{2,10},{10,18},{18,26},{... | collective-permute-start | bytes 1544 | tf_op jit(solution)/shard_map/ppermute | solution.py:26
  464.2 7.0 %collective-permute-start.87 = (f32[6,1,128]{2,0,1:T(8,128)S(1)}, f32[6,1,128]{2,0,1:T(8,128)S(1)}, u32[]{:S(2)}, u32[]{:S(2)}) collective-permute-start(f32[6,1,128]{2,0,1:T(8,128)S(1)} %pad_maximum_fusion.223), channel_id=1, source_target_pairs={{1,0},{2,1},{3,2},{4,3},{5,4},{6,5},{7,6},{9,8},{10,9},{11,10},{12... | collective-permute-start | bytes 9224 | tf_op jit(solution)/shard_map/ppermute | solution.py:27
  472.1 6.7 %collective-permute-start.90 = (f32[1,1,128]{2,0,1:T(1,128)S(1)}, f32[1,1,128]{2,0,1:T(1,128)S(1)}, u32[]{:S(2)}, u32[]{:S(2)}) collective-permute-start(f32[1,1,128]{2,0,1:T(1,128)S(1)} %get-tuple-element.90), channel_id=1, source_target_pairs={{8,0},{16,8},{24,16},{9,1},{17,9},{25,17},{10,2},{18,10},{26,18},{... | collective-permute-start | bytes 1544 | tf_op jit(solution)/shard_map/ppermute | solution.py:27
  473.4 6.1 %collective-permute-start.89 = (f32[1,1,128]{2,0,1:T(1,128)S(1)}, f32[1,1,128]{2,0,1:T(1,128)S(1)}, u32[]{:S(2)}, u32[]{:S(2)}) collective-permute-start(f32[1,1,128]{2,0,1:T(1,128)S(1)} %get-tuple-element.91), channel_id=1, source_target_pairs={{0,8},{8,16},{16,24},{1,9},{9,17},{17,25},{2,10},{10,18},{18,26},{... | collective-permute-start | bytes 1544 | tf_op jit(solution)/shard_map/ppermute | solution.py:26
  479.6 7.0 %collective-permute-start.91 = (f32[6,1,128]{2,0,1:T(8,128)S(1)}, f32[6,1,128]{2,0,1:T(8,128)S(1)}, u32[]{:S(2)}, u32[]{:S(2)}) collective-permute-start(f32[6,1,128]{2,0,1:T(8,128)S(1)} %pad_maximum_fusion.226), channel_id=1, source_target_pairs={{1,0},{2,1},{3,2},{4,3},{5,4},{6,5},{7,6},{9,8},{10,9},{11,10},{12... | collective-permute-start | bytes 9224 | tf_op jit(solution)/shard_map/ppermute | solution.py:27
  487.8 6.1 %collective-permute-start.93 = (f32[1,4,512]{2,1,0:T(4,128)S(1)}, f32[1,4,512]{2,1,0:T(4,128)S(1)}, u32[]{:S(2)}, u32[]{:S(2)}) collective-permute-start(f32[1,4,512]{2,1,0:T(4,128)S(1)} %get-tuple-element.75), channel_id=1, source_target_pairs={{0,8},{8,16},{16,24},{1,9},{9,17},{17,25},{2,10},{10,18},{18,26},{... | collective-permute-start | bytes 24584 | tf_op jit(solution)/shard_map/ppermute | solution.py:26
  498.5 7.3 %collective-permute-start.95 = (f32[6,1,512]{2,1,0:T(1,128)S(1)}, f32[6,1,512]{2,1,0:T(1,128)S(1)}, u32[]{:S(2)}, u32[]{:S(2)}) collective-permute-start(f32[6,1,512]{2,1,0:T(1,128)S(1)} %get-tuple-element.59), channel_id=1, source_target_pairs={{1,0},{2,1},{3,2},{4,3},{5,4},{6,5},{7,6},{9,8},{10,9},{11,10},{12... | collective-permute-start | bytes 36872 | tf_op jit(solution)/shard_map/ppermute | solution.py:27
  500.4 6.2 %collective-permute-start.96 = (f32[6,1,512]{2,1,0:T(1,128)S(1)}, f32[6,1,512]{2,1,0:T(1,128)S(1)}, u32[]{:S(2)}, u32[]{:S(2)}) collective-permute-start(f32[6,1,512]{2,1,0:T(1,128)S(1)} %get-tuple-element.58), channel_id=1, source_target_pairs={{0,1},{1,2},{2,3},{3,4},{4,5},{5,6},{6,7},{8,9},{9,10},{10,11},{11... | collective-permute-start | bytes 36872 | tf_op jit(solution)/shard_map/ppermute | solution.py:26
  515.8 7.6 %collective-permute-start.99 = (f32[6,1,512]{2,1,0:T(1,128)S(1)}, f32[6,1,512]{2,1,0:T(1,128)S(1)}, u32[]{:S(2)}, u32[]{:S(2)}) collective-permute-start(f32[6,1,512]{2,1,0:T(1,128)S(1)} %get-tuple-element.57), channel_id=1, source_target_pairs={{1,0},{2,1},{3,2},{4,3},{5,4},{6,5},{7,6},{9,8},{10,9},{11,10},{12... | collective-permute-start | bytes 36872 | tf_op jit(solution)/shard_map/ppermute | solution.py:27
  517.7 6.4 %collective-permute-start.100 = (f32[6,1,512]{2,1,0:T(1,128)S(1)}, f32[6,1,512]{2,1,0:T(1,128)S(1)}, u32[]{:S(2)}, u32[]{:S(2)}) collective-permute-start(f32[6,1,512]{2,1,0:T(1,128)S(1)} %get-tuple-element.56), channel_id=1, source_target_pairs={{0,1},{1,2},{2,3},{3,4},{4,5},{5,6},{6,7},{8,9},{9,10},{10,11},{11... | collective-permute-start | bytes 36872 | tf_op jit(solution)/shard_map/ppermute | solution.py:26
  539.1 7.6 %collective-permute-start.103 = (f32[6,1,2048]{2,1,0:T(1,128)S(1)}, f32[6,1,2048]{2,1,0:T(1,128)S(1)}, u32[]{:S(2)}, u32[]{:S(2)}) collective-permute-start(f32[6,1,2048]{2,1,0:T(1,128)S(1)} %get-tuple-element.21), channel_id=1, source_target_pairs={{1,0},{2,1},{3,2},{4,3},{5,4},{6,5},{7,6},{9,8},{10,9},{11,10},{12... | collective-permute-start | bytes 147464 | tf_op jit(solution)/shard_map/ppermute | solution.py:27
  541.0 6.8 %collective-permute-start.104 = (f32[6,1,2048]{2,1,0:T(1,128)S(1)}, f32[6,1,2048]{2,1,0:T(1,128)S(1)}, u32[]{:S(2)}, u32[]{:S(2)}) collective-permute-start(f32[6,1,2048]{2,1,0:T(1,128)S(1)} %get-tuple-element.20), channel_id=1, source_target_pairs={{0,1},{1,2},{2,3},{3,4},{4,5},{5,6},{6,7},{8,9},{9,10},{10,11},{11... | collective-permute-start | bytes 147464 | tf_op jit(solution)/shard_map/ppermute | solution.py:26
  557.3 7.6 %collective-permute-start.107 = (f32[6,1,2048]{2,1,0:T(1,128)S(1)}, f32[6,1,2048]{2,1,0:T(1,128)S(1)}, u32[]{:S(2)}, u32[]{:S(2)}) collective-permute-start(f32[6,1,2048]{2,1,0:T(1,128)S(1)} %get-tuple-element.19), channel_id=1, source_target_pairs={{1,0},{2,1},{3,2},{4,3},{5,4},{6,5},{7,6},{9,8},{10,9},{11,10},{12... | collective-permute-start | bytes 147464 | tf_op jit(solution)/shard_map/ppermute | solution.py:27
  559.3 6.8 %collective-permute-start.108 = (f32[6,1,2048]{2,1,0:T(1,128)S(1)}, f32[6,1,2048]{2,1,0:T(1,128)S(1)}, u32[]{:S(2)}, u32[]{:S(2)}) collective-permute-start(f32[6,1,2048]{2,1,0:T(1,128)S(1)} %get-tuple-element.18), channel_id=1, source_target_pairs={{0,1},{1,2},{2,3},{3,4},{4,5},{5,6},{6,7},{8,9},{9,10},{10,11},{11... | collective-permute-start | bytes 147464 | tf_op jit(solution)/shard_map/ppermute | solution.py:26
  575.7 7.6 %collective-permute-start.111 = (f32[6,1,2048]{2,1,0:T(1,128)S(1)}, f32[6,1,2048]{2,1,0:T(1,128)S(1)}, u32[]{:S(2)}, u32[]{:S(2)}) collective-permute-start(f32[6,1,2048]{2,1,0:T(1,128)S(1)} %get-tuple-element.17), channel_id=1, source_target_pairs={{1,0},{2,1},{3,2},{4,3},{5,4},{6,5},{7,6},{9,8},{10,9},{11,10},{12... | collective-permute-start | bytes 147464 | tf_op jit(solution)/shard_map/ppermute | solution.py:27
  577.6 6.8 %collective-permute-start.112 = (f32[6,1,2048]{2,1,0:T(1,128)S(1)}, f32[6,1,2048]{2,1,0:T(1,128)S(1)}, u32[]{:S(2)}, u32[]{:S(2)}) collective-permute-start(f32[6,1,2048]{2,1,0:T(1,128)S(1)} %get-tuple-element.16), channel_id=1, source_target_pairs={{0,1},{1,2},{2,3},{3,4},{4,5},{5,6},{6,7},{8,9},{9,10},{10,11},{11... | collective-permute-start | bytes 147464 | tf_op jit(solution)/shard_map/ppermute | solution.py:26
  (51 other events, 276.7 us)
where the time goes:
time: 596 us; the launch traced here: 587 us
  starting transfers between devices  351 us (59%)
  local copies, waits for them, and re-layouts  95.7 us (16%)
  waiting for transfers between devices  92.5 us (16%)
  other arithmetic  43.7 us (7%)
    ppermute x56, starting transfers between devices, padded_2(): before = lax.ppermute(last, axis, up)  255 us
    ppermute x56, starting transfers between devices, padded_2(): after = lax.ppermute(leading, axis, down)  91.7 us
    ppermute x56, waiting for transfers between devices, padded_2(): after = lax.ppermute(leading, axis, down)  58.9 us
    reshape x2, local copies, waits for them, and re-layouts, block_sums(): field.reshape(depth, height // 4, 4, lateral_extent // 4, 4)  37.4 us
    ppermute x56, waiting for transfers between devices, padded_2(): before = lax.ppermute(last, axis, up)  33.5 us
    concatenate x3, local copies, waits for them, and re-layouts, local(): lower_zero = jnp.concatenate([below[None], upper_zero[:-1]], axis=0)  30.6 us
    reduce_sum x10, other arithmetic, block_sums(): field.reshape(depth, height // 4, 4, lateral_extent // 4, 4)  23.3 us
  transfers between devices with their start and end apart: 113, of which 59 were waited for; matrix products, arithmetic and copies ran while one was open for 9% of the time, Pallas kernels for 0%

commit v1 on v0

v1 whole, which is shorter than its diff:
```python
import functools

import jax
import jax.numpy as jnp
import numpy as np
from jax import lax
from jax.experimental import pallas as pl
from jax.experimental.pallas import tpu as pltpu
from jax.sharding import PartitionSpec as P

OMEGA = 0.8
NC = 6
LN = 128
HX = 64
HY = 8
F32 = jnp.float32
BF16 = jnp.bfloat16


def iota(shape, axis):
    return lax.broadcasted_iota(jnp.int32, shape, axis)


def split_dot(x, m):
    hi = x.astype(BF16)
    lo = (x - hi.astype(F32)).astype(BF16)
    return jnp.dot(hi, m, preferred_element_type=F32) + jnp.dot(lo, m, preferred_element_type=F32)


def pair_dot(a, b):
    return lax.dot_general(a, b, (((0,), (0,)), ((), ())), preferred_element_type=F32)


class Sizes:
    def __init__(self, mesh_shape, f_shape, n_blocks):
        self.nd, self.nt = mesh_shape["die"], mesh_shape["tile"]
        self.lz, self.rows, self.width = f_shape
        self.nb = n_blocks
        self.wc = self.width // self.nd
        self.we = self.wc + LN
        self.nz = self.nd * self.lz
        self.re = self.rows + 2 * HY
        self.r1 = self.re // 4
        self.c1 = self.wc // 4
        self.e1 = 2 * self.r1
        self.w1 = 2 * LN
        self.c2 = self.wc // 16
        self.chunk = self.lz
        assert self.rows == 16 and self.lz == 4 and self.c1 == LN
        assert self.nd * self.c2 == LN and self.nb % 8 == 0 and self.nt <= LN


def pack_kernel(s, idx, mat, material, conductance, blocks, f, *outs):
    d = idx[0]
    lane, sub = iota((8, LN), 1), iota((8, LN), 0)
    info = jnp.where(lane == 1, conductance[0], 0.0)
    for z in range(s.lz):
        info = jnp.where((lane == 0) & (sub == z), mat[material[z]], info)
    low = lax.broadcasted_iota(jnp.int32, (s.rows, LN), 1) < HX
    n = s.lz * s.rows
    for step, out in enumerate(outs):
        e = lax.rem(d + step, s.nd)
        right = lax.rem(e + 1, s.nd) * s.wc
        left = lax.rem(e + s.nd - 1, s.nd) * s.wc + (s.wc - LN)
        for z in range(s.lz):
            rows = slice(z * s.rows, (z + 1) * s.rows)
            out[rows, : s.wc] = f[z, :, pl.ds(pl.multiple_of(e * s.wc, LN), s.wc)]
            out[rows, s.wc :] = jnp.where(
                low,
                f[z, :, pl.ds(pl.multiple_of(right, LN), LN)],
                f[z, :, pl.ds(pl.multiple_of(left, LN), LN)],
            )
        out[n:, :] = jnp.zeros((8, s.we), F32)
        for k in range(s.nb // 8):
            out[n:, k * LN : k * LN + 4] = blocks[8 * k : 8 * k + 8, :].astype(F32)
        k = s.nb // 8
        out[n:, k * LN : (k + 1) * LN] = info


def assemble_kernel(s, idx, *refs):
    parts, (top, bot, prm) = refs[: s.nd], refs[s.nd :]
    d = idx[0]
    for step, part in enumerate(parts):
        e = lax.rem(d + s.nd - step, s.nd)
        for z in range(s.lz):
            top[s.lz * e + z] = part[z * s.rows : z * s.rows + HY, :]
            bot[s.lz * e + z] = part[z * s.rows + HY : (z + 1) * s.rows, :]
        prm[e] = part[s.lz * s.rows :, :]


def overlap(lo, size, first, past):
    return jnp.maximum(jnp.minimum(lo + size, past) - jnp.maximum(lo, first), 0.0)


def coeff_kernel(s, idx, prm, u0, d0, u1, d1, u2, l2, d2, c, c2):
    d, t = idx[0], idx[1]
    ny = s.rows * s.nt
    lane8, sub8 = iota((8, LN), 1), iota((8, LN), 0)

    def pick(tile, row, col):
        return jnp.sum(jnp.where((lane8 == col) & (sub8 == row), tile, 0.0), keepdims=True)

    info = [prm[g, :, s.nb // 8 * LN : (s.nb // 8 + 1) * LN] for g in range(s.nd)]
    cond = [pick(info[z // s.lz], z % s.lz, 0) for z in range(s.nz)]
    via = [pick(info[g], 0, 1) for g in range(s.nd)]
    vert = [
        2.0 * cond[z] * cond[min(z + 1, s.nz - 1)] / (cond[z] + cond[min(z + 1, s.nz - 1)])
        for z in range(s.nz)
    ]
    lane = iota((s.nb, LN), 1)
    blocks = []
    for g in range(s.nd):
        b = jnp.concatenate([prm[g, :, k * LN : (k + 1) * LN] for k in range(s.nb // 8)], axis=0)
        col = [jnp.sum(jnp.where(lane == j, b, 0.0), axis=1, keepdims=True) for j in range(4)]
        blocks.append((col[0], col[0] + col[2], col[1], col[1] + col[3]))

    p0 = iota((1, s.we), 1)
    col0 = d * s.wc + p0 - jnp.where(p0 >= s.wc + HX, s.we, 0)
    p1 = iota((1, s.w1), 1)
    col1 = d * s.c1 + p1 - jnp.where(p1 >= s.w1 - HX // 4, s.w1, 0)
    used1 = (p1 < s.c1 + HX // 4) | (p1 >= s.w1 - HX // 4)
    row0 = t * s.rows - HY + iota((1, LN), 1)
    row1 = t * (s.rows // 4) - (s.e1 - s.rows // 4) // 2 + iota((1, LN), 1)
    zero0 = jnp.zeros((s.re, s.we), F32)
    zero1 = jnp.zeros((s.e1, s.w1), F32)
    u0[0] = zero0
    u1[0] = zero1
    for z in range(s.nz):
        g = z // s.lz
        if z % s.lz == s.lz - 1:
            r0, r1, c0, c1 = blocks[g]
            a = overlap(row0.astype(F32), 1.0, r0, r1).astype(BF16)
            b = overlap(col0.astype(F32), 1.0, c0, c1).astype(BF16)
            u0[z + 1] = pair_dot(a, b)[: s.re] * via[g]
            a = overlap(row1.astype(F32) * 4.0, 4.0, r0, r1).astype(BF16)
            b = overlap(col1.astype(F32) * 4.0, 4.0, c0, c1).astype(BF16)
            u1[z + 1] = pair_dot(a, b)[: s.e1] * via[g]
        else:
            u0[z + 1] = zero0 + vert[z]
            u1[z + 1] = zero1 + vert[z] * 16.0
        c[z] = jnp.zeros((8, LN), F32) + cond[z]
    rr = t * s.rows - HY + iota((s.re, s.we), 0)
    pp = iota((s.re, s.we), 1)
    cc = d * s.wc + pp - jnp.where(pp >= s.wc + HX, s.we, 0)
    in0 = jnp.where((rr >= 0) & (rr < ny) & (cc >= 0) & (cc < s.width), OMEGA, 0.0)
    rr = t * (s.rows // 4) - (s.e1 - s.rows // 4) // 2 + iota((s.e1, s.w1), 0)
    pp = iota((s.e1, s.w1), 1)
    cc = d * s.c1 + pp - jnp.where(pp >= s.w1 - HX // 4, s.w1, 0)
    in1 = (rr >= 0) & (rr < ny // 4) & (cc >= 0) & (cc < s.width // 4)
    in1 = jnp.where(in1 & ((pp < s.c1 + HX // 4) | (pp >= s.w1 - HX // 4)), OMEGA, 0.0)
    for z in range(s.nz):
        d0[z] = in0 / (4.0 * cond[z] + u0[z + 1] + u0[z])
        d1[z] = in1 / (16.0 * cond[z] + u1[z + 1] + u1[z])

    group = iota((1, LN), 1) // s.c2
    xin = iota((1, LN), 1) % s.c2

    def by_group(values):
        out = jnp.zeros((1, LN), F32)
        for g in range(s.nd):
            out = jnp.where(group == g, values[g], out)
        return out

    cl = [by_group([cond[s.lz * g + a] for g in range(s.nd)]) * 16.0 for a in range(s.lz)]
    vl = [by_group([vert[s.lz * g + a] for g in range(s.nd)]) * 256.0 for a in range(s.lz)]
    vial = by_group(via)
    row2 = (iota((1, LN), 1) * 16).astype(F32)
    ra = jnp.concatenate([overlap(row2, 16.0, b[0], b[1]) for b in blocks], axis=0).astype(BF16)
    zero2 = jnp.zeros((s.nt, LN), F32)
    for a in range(s.lz):
        c2[a] = jnp.zeros((8, LN), F32) + cl[a]
    for e in range(s.nd):
        col2 = ((e * s.c2 + xin) * 16).astype(F32)
        cb = jnp.concatenate(
            [jnp.where(group == g, overlap(col2, 16.0, b[2], b[3]), 0.0) for g, b in enumerate(blocks)],
            axis=0,
        ).astype(BF16)
        v2 = pair_dot(ra, cb)[: s.nt] * vial
        ups = [zero2 + vl[a] for a in range(s.lz - 1)] + [v2]
        first = jnp.where(iota((s.nt, LN), 1) >= s.c2, pltpu.roll(v2, s.c2, 1), 0.0)
        lows = [first] + ups[:-1]
        for a in range(s.lz):
            q = e * s.lz + a
            u2[q] = ups[a]
            l2[q] = lows[a]
            d2[q] = OMEGA / (4.0 * cl[a] + ups[a] + lows[a])


def neighbours(v, c):
    rows, cols = v.shape
    side = (
        pltpu.roll(v, 1, 0) + pltpu.roll(v, rows - 1, 0) + (pltpu.roll(v, 1, 1) + pltpu.roll(v, cols - 1, 1))
    )
    return c * side


def off_diagonal(src, z, u, c, scale):
    v = src[z + 1]
    return v, neighbours(v, c[z, 0:1, 0:1] * scale) + u[z + 1] * src[z + 2] + u[z] * src[z]


def sweep(s, src, dst, f, u, dd, c, scale):
    def body(z, carry):
        v, g = off_diagonal(src, z, u, c, scale)
        dst[z + 1] = (1.0 - OMEGA) * v + dd[z] * (f[z] + g)
        return carry

    lax.fori_loop(0, s.nz, body, 0)


def residual(src, z, f, u, c, scale):
    v, g = off_diagonal(src, z, u, c, scale)
    return f[z] + g - (4.0 * scale * c[z, 0:1, 0:1] + u[z + 1] + u[z]) * v


def zero_ends(s, *bufs):
    for b in bufs:
        b[0] = jnp.zeros(b.shape[1:], F32)
        b[s.nz + 1] = jnp.zeros(b.shape[1:], F32)


def restrict(s, src, f, u, c, down, row_buf, sums, r1):
    def body(z, carry):
        r = residual(src, z, f, u, c, 1.0)
        at = pl.ds(pl.multiple_of(z * s.r1, 8), s.r1)
        for j in range(s.we // LN):
            row_buf[j * s.re : (j + 1) * s.re, :] = r[:, j * LN : (j + 1) * LN]
        for j in range(s.we // LN):
            part = [row_buf[pl.ds(j * s.re + k, s.r1, stride=4), :] for k in range(4)]
            sums[at, j * LN : (j + 1) * LN] = (part[0] + part[1]) + (part[2] + part[3])
        return carry

    lax.fori_loop(0, s.nz, body, 0)
    r1[...] = split_dot(sums[...], down[...]).reshape(s.nz, s.r1, s.w1)


def fine_first_kernel(s, above, top, bot, below, u0, d0, c, down, f, v2, r1, va, row_buf, sums):
    zero_ends(s, va, v2)

    def body(z, carry):
        for k, ref in enumerate((above, top, bot, below)):
            rows = slice(k * HY, (k + 1) * HY)
            x = ref[z]
            f[z, rows, :] = x
            va[z + 1, rows, :] = d0[z, rows, :] * x
        return carry

    lax.fori_loop(0, s.nz, body, 0)
    sweep(s, va, v2, f, u0, d0, c, 1.0)
    restrict(s, v2, f, u0, c, down, row_buf, sums, r1)


def middle_first_kernel(s, r1p, r1, r1n, u1, d1, c, down2, rx, w2, send, wa, gather):
    own = s.rows // 4
    pad = (s.e1 - own) // 2
    sub = iota((s.r1, s.w1), 0)
    zero_ends(s, wa, w2)

    def body(z, carry):
        mid = pltpu.roll(r1[z], s.r1 // 2, 0)
        up = jnp.where(sub >= pad, mid, r1p[z])
        down = jnp.where(sub < own - (s.r1 - pad), mid, r1n[z])
        rx[z, : s.r1, :] = up
        rx[z, s.r1 :, :] = down
        wa[z + 1, : s.r1, :] = d1[z, : s.r1, :] * up
        wa[z + 1, s.r1 :, :] = d1[z, s.r1 :, :] * down
        return carry

    lax.fori_loop(0, s.nz, body, 0)
    sweep(s, wa, w2, rx, u1, d1, c, 4.0)
    row = iota((s.e1, LN), 0)
    mine = (row >= pad) & (row < pad + own)
    for z in range(s.nz):
        r = residual(w2, z, rx, u1, c, 4.0)[:, :LN]
        total = jnp.sum(jnp.where(mine, r, 0.0), axis=0, keepdims=True)
        g, a = z // s.lz, z % s.lz
        gather[a : a + 1, g * LN : (g + 1) * LN] = total
        gather[a + s.lz : a + s.lz + 1, g * LN : (g + 1) * LN] = total
    tile = split_dot(gather[...], down2[...])
    for k in range(s.nd * s.nt * s.chunk // 8):
        send[8 * k : 8 * k + 8, :] = tile


def coarse(s, got, u2, l2, d2, c2, cs):
    lane = iota((s.nt, LN), 1)
    x, t = lane % s.c2, iota((s.nt, LN), 0)
    first_x, last_x = x == 0, x == s.c2 - 1
    slabs = s.nd * s.lz
    rhs, v = [], []
    for q in range(slabs):
        e, a = q // s.lz, q % s.lz
        r = got[pl.ds(e * s.nt * s.lz + a, s.nt, stride=s.lz), :]
        rhs.append(r)
        v.append(d2[q] * r)
    zero = jnp.zeros((s.nt, LN), F32)

    def body(_, v):
        new = []
        for q in range(slabs):
            e, a = q // s.lz, q % s.lz
            w = v[q]
            right = pltpu.roll(v[q + s.lz], s.c2 - 1, 1) if e < s.nd - 1 else zero
            left = pltpu.roll(v[q - s.lz], LN - (s.c2 - 1), 1) if e > 0 else zero
            side = jnp.where(last_x, right, pltpu.roll(w, LN - 1, 1))
            side += jnp.where(first_x, left, pltpu.roll(w, 1, 1))
            side += jnp.where(t == s.nt - 1, 0.0, pltpu.roll(w, s.nt - 1, 0))
            side += jnp.where(t == 0, 0.0, pltpu.roll(w, 1, 0))
            if a < s.lz - 1:
                up = v[q + 1]
            else:
                up = jnp.where(lane >= LN - s.c2, 0.0, pltpu.roll(v[q - a], LN - s.c2, 1))
            if a > 0:
                down = v[q - 1]
            else:
                down = jnp.where(lane < s.c2, 0.0, pltpu.roll(v[q + s.lz - 1], s.c2, 1))
            g = c2[a, 0:1, :] * side + u2[q] * up + l2[q] * down
            new.append((1.0 - OMEGA) * w + d2[q] * (rhs[q] + g))
        return tuple(new)

    v = lax.fori_loop(0, NC - 1, body, tuple(v))
    for q in range(slabs):
        cs[q, : HY, :] = jnp.zeros((HY, LN), F32)
        cs[q, HY + s.nt :, :] = jnp.zeros((HY, LN), F32)
        cs[q, HY : HY + s.nt, :] = v[q]


def middle_last(s, d, t, cs, spread2, w2, rx, u1, d1, c, comp, wa, wb):
    own = s.rows // 4
    pad = (s.e1 - own) // 2
    row = iota((s.e1, LN), 0)
    lane = iota((s.e1, LN), 1)
    after = lax.rem(d + 1, s.nd) * s.lz
    before = lax.rem(d + s.nd - 1, s.nd) * s.lz
    zero_ends(s, wa, wb)
    for a in range(s.lz):
        rows = []
        for base in (d * s.lz, after, before):
            out = jnp.zeros((s.e1, LN), F32)
            for k in range(-2, 3):
                lo = pad + own * k
                line = cs[base + a, pl.ds(HY + t + k, 1), :]
                out = jnp.where((row >= lo) & (row < lo + own), line, out)
            rows.append(out)
        for g in range(s.nd):
            turn = [pltpu.roll(r, (sh - g * s.c2) % LN, 1) if (sh - g * s.c2) % LN else r
                    for r, sh in zip(rows, (0, s.c2, LN - s.c2))]
            z = g * s.lz + a
            comp[z * s.e1 : (z + 1) * s.e1, :] = jnp.where(
                lane < s.c2, turn[0], jnp.where(lane < LN // 2, turn[1], turn[2])
            )
    wa[1 : s.nz + 1] = split_dot(comp[...], spread2[...]).reshape(s.nz, s.e1, s.w1)

    def body(z, carry):
        wa[z + 1] = jnp.where(d1[z] > 0.0, w2[z + 1] + wa[z + 1], 0.0)
        return carry

    lax.fori_loop(0, s.nz, body, 0)
    sweep(s, wa, wb, rx, u1, d1, c, 4.0)
    sweep(s, wb, wa, rx, u1, d1, c, 4.0)


def correct_fine(s, w, v, spread1, wide, dst):
    first = (s.e1 - s.r1) // 2
    lhs = w[1 : s.nz + 1, first : first + s.r1, :].reshape(s.nz * s.r1, s.w1)
    wide[...] = split_dot(lhs, spread1[...])
    zero_ends(s, dst)
    upper = iota((8, s.we), 0) < 4

    def body(z, carry):
        x = wide[pl.ds(pl.multiple_of(z * s.r1, 8), s.r1), :]
        for k in range(s.r1 // 2):
            rows = slice(8 * k, 8 * k + 8)
            step = jnp.where(upper, x[2 * k : 2 * k + 1, :], x[2 * k + 1 : 2 * k + 2, :])
            dst[z + 1, rows, :] = v[z + 1, rows, :] + step
        return carry

    lax.fori_loop(0, s.nz, body, 0)


def back_kernel(
    s, idx, got, u2, l2, d2, c2, w2, rx, u1, d1, c, v2, f, u0, d0, spread2, spread1, down,
    v, r1, cs, comp, wa, wb, va, wide, row_buf,
):
    d, t = idx[0], idx[1]
    coarse(s, got, u2, l2, d2, c2, cs)
    middle_last(s, d, t, cs, spread2, w2, rx, u1, d1, c, comp, wa, wb)
    correct_fine(s, wa, v2, spread1, wide, va)
    zero_ends(s, v)
    sweep(s, va, v, f, u0, d0, c, 1.0)
    sweep(s, v, va, f, u0, d0, c, 1.0)
    sweep(s, va, v, f, u0, d0, c, 1.0)
    sweep(s, v, va, f, u0, d0, c, 1.0)

    def body(z, carry):
        v[z + 1] = va[z + 1]
        return carry

    lax.fori_loop(0, s.nz, body, 0)
    restrict(s, va, f, u0, c, down, row_buf, wide, r1)


def last_kernel(
    s, idx, got, u2, l2, d2, c2, w2, rx, u1, d1, c, v2, f, u0, d0, spread2, spread1,
    *refs,
):
    outs, (cs, comp, wa, wb, va, vb, wide) = refs[: s.nd], refs[s.nd :]
    d, t = idx[0], idx[1]
    coarse(s, got, u2, l2, d2, c2, cs)
    middle_last(s, d, t, cs, spread2, w2, rx, u1, d1, c, comp, wa, wb)
    correct_fine(s, wa, v2, spread1, wide, va)
    zero_ends(s, vb)
    sweep(s, va, vb, f, u0, d0, c, 1.0)
    sweep(s, vb, va, f, u0, d0, c, 1.0)
    for step, out in enumerate(outs):
        e = lax.rem(d + step, s.nd)
        for a in range(s.lz):
            z = e * s.lz + a
            out[0, a] = va[z + 1, HY : HY + s.rows, : s.wc]
            out[1, a] = residual(va, z, f, u0, c, 1.0)[HY : HY + s.rows, : s.wc]


def unpack_kernel(s, idx, *refs):
    parts, outs = refs[: s.nd], refs[s.nd :]
    d = idx[0]
    for step, part in enumerate(parts):
        e = lax.rem(d + s.nd - step, s.nd)
        cols = pl.ds(pl.multiple_of(e * s.wc, LN), s.wc)
        for k, out in enumerate(outs):
            for a in range(s.lz):
                out[a, :, cols] = part[k, a]


def call(name, kernel, s, n_smem, outs, scratch=(), flops=0):
    shapes = [jax.ShapeDtypeStruct(o, F32) for o in outs]
    vm = pl.BlockSpec(memory_space=pltpu.VMEM)

    def run(*args):
        total = sum(int(np.prod(a.shape)) * 4 for a in args) + sum(int(np.prod(o)) * 4 for o in outs)
        return pl.pallas_call(
            functools.partial(kernel, s),
            name=name,
            out_shape=shapes,
            in_specs=[pl.BlockSpec(memory_space=pltpu.SMEM)] * n_smem + [vm] * (len(args) - n_smem),
            out_specs=[vm] * len(outs),
            scratch_shapes=[pltpu.VMEM(x, F32) for x in scratch],
            compiler_params=pltpu.CompilerParams(vmem_limit_bytes=32 << 20),
            cost_estimate=pl.CostEstimate(flops=flops, bytes_accessed=total, transcendentals=0),
        )(*args)

    return run


def shift(x, axis, by):
    n = lax.axis_size(axis)
    return lax.ppermute(x, axis, [(i, (i + by) % n) for i in range(n)])


def tables(s):
    p = np.arange(s.we)
    at = p // 4 + np.where(p >= s.wc + HX, s.w1 - s.we // 4, 0)
    down = (at[:, None] == np.arange(s.w1)[None, :])
    q = np.arange(s.w1)
    k = q // 4 + np.where(q >= s.w1 - HX // 4, LN - s.w1 // 4, 0)
    used = (q < s.c1 + HX // 4) | (q >= s.w1 - HX // 4)
    spread2 = (np.arange(LN)[:, None] == k[None, :]) & used[None, :]
    r = np.arange(s.nd * LN)
    down2 = ((r // LN) * s.c2 + (r % LN) // 4)[:, None] == np.arange(LN)[None, :]
    return [jnp.asarray(m, BF16) for m in (down, down.T, spread2, down2)]


def local(s, source_heating, material_thermal_values, layer_material, via_conductance, via_blocks):
    idx = jnp.stack([lax.axis_index("die"), lax.axis_index("tile")]).astype(jnp.int32)
    down, spread1, spread2, down2 = tables(s)
    packed = (s.lz * s.rows + 8, s.we)
    sends = call("pack", pack_kernel, s, 4, [packed] * s.nd)(
        idx, material_thermal_values, layer_material, via_conductance, via_blocks[0], source_heating
    )
    parts = [sends[0]] + [shift(sends[k], "die", k) for k in range(1, s.nd)]
    half = (s.nz, HY, s.we)
    top, bot, prm = call("assemble", assemble_kernel, s, 1, [half, half, (s.nd, 8, s.we)])(idx, *parts)
    above, below = shift(bot, "tile", 1), shift(top, "tile", -1)
    fine, fine_v = (s.nz, s.re, s.we), (s.nz + 2, s.re, s.we)
    mid, mid_v, mid_u = (s.nz, s.e1, s.w1), (s.nz + 2, s.e1, s.w1), (s.nz + 1, s.e1, s.w1)
    small = (s.nz, s.r1, s.w1)
    flat = (s.nz * s.r1, s.we)
    rows_buf = (s.re * s.we // LN, LN)
    slab = (s.nd * s.lz, s.nt, LN)
    u0, d0, u1, d1, u2, l2, d2, c, c2 = call(
        "coeff", coeff_kernel, s, 1,
        [(s.nz + 1, s.re, s.we), fine, mid_u, mid, slab, slab, slab, (s.nz, 8, LN), (s.lz, 8, LN)],
    )(idx, prm)
    f, v, r1 = call(
        "fine_first", fine_first_kernel, s, 0, [fine, fine_v, small], [fine_v, rows_buf, flat]
    )(above, top, bot, below, u0, d0, c, down)
    spaces = [(s.nd * s.lz, s.nt + 2 * HY, LN), (s.nz * s.e1, LN), mid_v, mid_v, fine_v]
    for cycle in range(2):
        rx, w2, send = call(
            "middle_first", middle_first_kernel, s, 0,
            [mid, mid_v, (s.nd * s.nt * s.chunk, LN)], [mid_v, (8, s.nd * LN)],
        )(shift(r1, "tile", 1), r1, shift(r1, "tile", -1), u1, d1, c, down2)
        got = lax.all_to_all(send, ("die", "tile"), 0, 0, tiled=True)
        args = (idx, got, u2, l2, d2, c2, w2, rx, u1, d1, c, v, f, u0, d0, spread2, spread1)
        if cycle == 0:
            v, r1 = call(
                "back", back_kernel, s, 1, [fine_v, small], spaces + [flat, rows_buf]
            )(*args, down)
    piece = (2, s.lz, s.rows, s.wc)
    sends = call("last", last_kernel, s, 1, [piece] * s.nd, spaces + [fine_v, flat])(*args)
    parts = [sends[0]] + [shift(sends[k], "die", k) for k in range(1, s.nd)]
    whole = (s.lz, s.rows, s.width)
    return tuple(call("unpack", unpack_kernel, s, 1, [whole, whole])(idx, *parts))


def solution(mesh):
    in_specs = (P("die", "tile", None), P(), P("die"), P("die"), P("die", None, None))
    out_specs = (P("die", "tile", None), P("die", "tile", None))

    def body(f, mat, material, conductance, blocks):
        s = Sizes(mesh.shape, f.shape, blocks.shape[1])
        return local(s, f, mat, material, conductance, blocks)

    return jax.shard_map(body, mesh=mesh, in_specs=in_specs, out_specs=out_specs, check_vma=False)
```

time: 596 us -> 115 us (0.19); the launches traced: 587 us -> 114 us
  starting transfers between devices: 351 us -> 12.7 us
  local copies, waits for them, and re-layouts: 95.7 us -> 3.13 us
  waiting for transfers between devices: 92.5 us -> 32.3 us
  other arithmetic: 43.7 us -> 0.07 us
  Pallas kernels: 0 us -> 39.8 us
  blocking collectives: 0 us -> 24 us
    ppermute x113 -> x12, starting transfers between devices: 351 us -> 12.7 us  [shift(): return lax.ppermute(x, axis, [(i, (i + by) % n) for i in range(n)])]
    ppermute x113 -> x12, waiting for transfers between devices: 92.5 us -> 32.3 us  [shift(): return lax.ppermute(x, axis, [(i, (i + by) % n) for i in range(n)])]
    reshape x6 -> x0, local copies, waits for them, and re-layouts: 43.6 us -> none  [the longest x2 37.4 us: block_sums(): field.reshape(depth, height // 4, 4, lateral_extent // 4, 4)]
    pallas_call x0 -> x9, Pallas kernels: none -> 39.8 us  [run(): pl.pallas_call(functools.partial(kernel, s), name=name, out_shape=shapes,...]
    concatenate x3 -> x0, local copies, waits for them, and re-layouts: 30.6 us -> none  [local(): lower_zero = jnp.concatenate([below[None], upper_zero[:-1]], axis=0)]
    reduce_sum x11 -> x0, other arithmetic: 24.2 us -> none  [the longest x10 23.3 us: block_sums(): field.reshape(depth, height // 4, 4, lateral_extent // 4, 4)]
    all_to_all x0 -> x2, blocking collectives: none -> 24 us  [local(): got = lax.all_to_all(send, ('die', 'tile'), 0, 0, tiled=True)]
    broadcast_in_dim x10 -> x0, local copies, waits for them, and re-layouts: 14.7 us -> none  [the longest x2 8.57 us: local(): jnp.where(placed_above[:, None, None], via_plane[None], vertical[:, None,...]
  transfers between devices with their start and end apart: 113 -> 12, of which waited for: 59 -> 9; matrix products, arithmetic and copies ran while one was open for 9% -> 0% of each run, Pallas kernels for 0% -> 1%
where the time goes in v1:
time: 115 us; the launch traced here: 114 us
  Pallas kernels  39.8 us (35%)
  waiting for transfers between devices  32.3 us (28%)
  blocking collectives  24 us (21%)
  starting transfers between devices  12.7 us (11%)
  local copies, waits for them, and re-layouts  3.13 us (3%)
  between operations  1.43 us (1%)
    pallas_call x9, Pallas kernels, run(): pl.pallas_call(functools.partial(kernel, s), name=name, out_shape=shapes,...  39.8 us
    ppermute x12, waiting for transfers between devices, shift(): return lax.ppermute(x, axis, [(i, (i + by) % n) for i in range(n)])  32.3 us
    all_to_all x2, blocking collectives, local(): got = lax.all_to_all(send, ('die', 'tile'), 0, 0, tiled=True)  24 us
    ppermute x12, starting transfers between devices, shift(): return lax.ppermute(x, axis, [(i, (i + by) % n) for i in range(n)])  12.7 us
    unnamed x14, local copies, waits for them, and re-layouts  2.37 us
  transfers between devices with their start and end apart: 12, of which 9 were waited for; matrix products, arithmetic and copies ran while one was open for 0% of the time, Pallas kernels for 1%

profile of v1, /device:TPU:1, one launch (start us, length us, event | category | flops | bytes accessed | tf_op | source)
XLA Modules:
  0.0 113.5 jit_solution(9603670583246885414)
XLA Ops:
  0.6 0.0 copy-start
  1.3 0.8 copy.11.blocks
  2.1 0.1 pad_add_fusion.idx
  2.2 0.0 copy-start.3
  2.2 1.0 copy-done.3
  3.2 0.0 copy-start.5
  3.2 0.7 copy-done.5
  3.9 0.0 copy-start.6
  3.9 0.7 copy-done.6
  4.5 0.6 pack.1
  5.2 2.1 %collective-permute-start = (f32[72,640]{1,0:T(8,128)S(1)}, f32[72,640]{1,0:T(8,128)S(1)}, u32[]{:S(2)}, u32[]{:S(2)}) collective-permute-start(f32[72,640]{1,0:T(8,128)S(1)} %get-tuple-element.34), channel_id=1, source_target_pairs={{0,8},{8,16},{16,24},{24,0},{1,9},{9,17},{17,25},{25,1},{2,10},{10... | collective-permute-start | bytes 552968 | tf_op jit(solution)/shard_map/ppermute | solution.py:455
  7.2 1.2 %collective-permute-start.1 = (f32[72,640]{1,0:T(8,128)S(1)}, f32[72,640]{1,0:T(8,128)S(1)}, u32[]{:S(2)}, u32[]{:S(2)}) collective-permute-start(f32[72,640]{1,0:T(8,128)S(1)} %get-tuple-element.35), channel_id=1, source_target_pairs={{0,16},{8,24},{16,0},{24,8},{1,17},{9,25},{17,1},{25,9},{2,18},{10... | collective-permute-start | bytes 552968 | tf_op jit(solution)/shard_map/ppermute | solution.py:455
  8.5 1.2 %collective-permute-start.2 = (f32[72,640]{1,0:T(8,128)S(1)}, f32[72,640]{1,0:T(8,128)S(1)}, u32[]{:S(2)}, u32[]{:S(2)}) collective-permute-start(f32[72,640]{1,0:T(8,128)S(1)} %get-tuple-element.36), channel_id=1, source_target_pairs={{0,24},{8,0},{16,8},{24,16},{1,25},{9,1},{17,9},{25,17},{2,26},{10... | collective-permute-start | bytes 552968 | tf_op jit(solution)/shard_map/ppermute | solution.py:455
  9.6 2.9 %collective-permute-done.refs_1_ = f32[72,640]{1,0:T(8,128)S(1)} collective-permute-done((f32[72,640]{1,0:T(8,128)S(1)}, f32[72,640]{1,0:T(8,128)S(1)}, u32[]{:S(2)}, u32[]{:S(2)}) %collective-permute-start) | collective-permute-done | bytes 184352 | tf_op jit(solution)/shard_map/ppermute | solution.py:455
  12.6 4.7 %collective-permute-done.1.refs_2_ = f32[72,640]{1,0:T(8,128)S(1)} collective-permute-done((f32[72,640]{1,0:T(8,128)S(1)}, f32[72,640]{1,0:T(8,128)S(1)}, u32[]{:S(2)}, u32[]{:S(2)}) %collective-permute-start.1) | collective-permute-done | bytes 184352 | tf_op jit(solution)/shard_map/ppermute | solution.py:455
  17.2 0.0 collective-permute-done.2.refs_3_
  17.3 0.6 assemble.1
  17.9 2.0 %collective-permute-start.3 = (f32[16,8,640]{2,1,0:T(8,128)S(1)}, f32[16,8,640]{2,1,0:T(8,128)S(1)}, u32[]{:S(2)}, u32[]{:S(2)}) collective-permute-start(f32[16,8,640]{2,1,0:T(8,128)S(1)} %get-tuple-element.37.bot), channel_id=1, source_target_pairs={{0,1},{1,2},{2,3},{3,4},{4,5},{5,6},{6,7},{7,0},{8,9},{9,10},{10,1... | collective-permute-start | bytes 983048 | tf_op jit(solution)/shard_map/ppermute | solution.py:455
  19.9 0.0 collective-permute-start.4
  19.9 1.5 %coeff.1 = (f32[17,32,640]{2,1,0:T(8,128)S(1)}, f32[16,32,640]{2,1,0:T(8,128)S(1)}, f32[17,16,256]{2,1,0:T(8,128)S(1)}, f32[16,16,256]{2,1,0:T(8,128)S(1)}, f32[...) custom-call(s32[2]{0:T(128)S(1)} %pad_add_fusion.idx, ...), custom_call_target="tpu_custom_call" | custom-call | bytes 3604488 | tf_op jit(solution)/shard_map/coeff/pallas_call | solution.py:439
  21.4 3.5 %collective-permute-done.3.above = f32[16,8,640]{2,1,0:T(8,128)S(1)} collective-permute-done((f32[16,8,640]{2,1,0:T(8,128)S(1)}, f32[16,8,640]{2,1,0:T(8,128)S(1)}, u32[]{:S(2)}, u32[]{:S(2)}) %collective-permute-start.3) | collective-permute-done | bytes 327712 | tf_op jit(solution)/shard_map/ppermute | solution.py:455
  24.9 5.0 %collective-permute-done.4.below = f32[16,8,640]{2,1,0:T(8,128)S(1)} collective-permute-done((f32[16,8,640]{2,1,0:T(8,128)S(1)}, f32[16,8,640]{2,1,0:T(8,128)S(1)}, u32[]{:S(2)}, u32[]{:S(2)}) %collective-permute-start.4) | collective-permute-done | bytes 327712 | tf_op jit(solution)/shard_map/ppermute | solution.py:455
  29.8 0.0 copy-done
  29.8 0.0 copy-start.2
  29.8 0.0 copy-start.4
  29.8 5.1 %fine_first.1 = (f32[16,32,640]{2,1,0:T(8,128)S(1)}, f32[18,32,640]{2,1,0:T(8,128)S(1)}, f32[16,8,256]{2,1,0:T(8,128)S(1)}) custom-call(f32[16,8,640]{2,1,0:T(8,128)S(1)} %collective-permute-done.3.above, f32[16,8,640]{2,1,0:T(8,128)S(1)} %get-tuple-element.38.top, f32[16,8,640]{2,1,0:T(8,128)S(1)} %get-tuple-element.37.bot, ...), custom_call_target="tpu_custom_call" | custom-call | bytes 7651328 | tf_op jit(solution)/shard_map/fine_first/pallas_call | solution.py:439
  34.9 0.0 copy-start.1
  35.0 0.1 collective-permute-start.6
  35.0 1.7 %collective-permute-start.5 = (f32[16,8,256]{2,1,0:T(8,128)S(1)}, f32[16,8,256]{2,1,0:T(8,128)S(1)}, u32[]{:S(2)}, u32[]{:S(2)}) collective-permute-start(f32[16,8,256]{2,1,0:T(8,128)S(1)} %get-tuple-element.43.r1), channel_id=1, source_target_pairs={{0,1},{1,2},{2,3},{3,4},{4,5},{5,6},{6,7},{7,0},{8,9},{9,10},{10,1... | collective-permute-start | bytes 393224 | tf_op jit(solution)/shard_map/ppermute | solution.py:455
  36.8 2.6 %collective-permute-done.6.r1n = f32[16,8,256]{2,1,0:T(8,128)S(1)} collective-permute-done((f32[16,8,256]{2,1,0:T(8,128)S(1)}, f32[16,8,256]{2,1,0:T(8,128)S(1)}, u32[]{:S(2)}, u32[]{:S(2)}) %collective-permute-start.6) | collective-permute-done | bytes 131104 | tf_op jit(solution)/shard_map/ppermute | solution.py:455
  39.4 0.4 collective-permute-done.5.r1p
  39.8 0.0 copy-done.2
  39.8 1.8 %middle_first.2 = (f32[16,16,256]{2,1,0:T(8,128)S(1)}, f32[18,16,256]{2,1,0:T(8,128)S(1)}, f32[128,128]{1,0:T(8,128)S(1)}) custom-call(f32[16,8,256]{2,1,0:T(8,128)S(1)} %collective-permute-done.5.r1p, f32[16,8,256]{2,1,0:T(8,128)S(1)} %get-tuple-element.43.r1, f32[16,8,256]{2,1,0:T(8,128)S(1)} %collective-permute-done.6.r1n, ...), custom_call_target="tpu_custom_call" | custom-call | bytes 1884160 | tf_op jit(solution)/shard_map/middle_first/pallas_call | solution.py:439
  41.7 12.6 %all_to_all.22 = f32[32,4,128]{2,1,0:T(4,128)S(1)} all-to-all(f32[32,4,128]{2,1,0:T(4,128)S(1)} %bitcast.10), channel_id=1, replica_groups=mesh['die'=4,'tile'=8] {'die','tile'}, dimensions={0} | all-to-all | bytes 131072 | tf_op jit(solution)/shard_map/all_to_all | solution.py:501
  54.3 0.0 copy-done.4
  54.3 0.0 copy-done.1
  54.4 16.7 %back.1 = (f32[18,32,640]{2,1,0:T(8,128)S(1)}, f32[16,8,256]{2,1,0:T(8,128)S(1)}) custom-call(s32[2]{0:T(128)S(1)} %pad_add_fusion.idx, f32[128,128]{1,0:T(8,128)S(1)} %bitcast.7, f32[16,8,128]{2,1,0:T(8,128)S(1)} %get-tuple-element.47.u2, f32[16,8,128]{2,1,0:T(8,128)S(1)} %get-tuple-element.48.l2, f32[16,8,128]{2,1,0:T(8,128)S(1)} %get-tuple-element.49.d2, ...), custom_call_target="tpu_custom_call" | custom-call | bytes 9977864 | tf_op jit(solution)/shard_map/back/pallas_call | solution.py:439
  71.1 0.4 collective-permute-start.8
  71.5 1.4 %collective-permute-start.7 = (f32[16,8,256]{2,1,0:T(8,128)S(1)}, f32[16,8,256]{2,1,0:T(8,128)S(1)}, u32[]{:S(2)}, u32[]{:S(2)}) collective-permute-start(f32[16,8,256]{2,1,0:T(8,128)S(1)} %get-tuple-element.55.r1), channel_id=1, source_target_pairs={{0,1},{1,2},{2,3},{3,4},{4,5},{5,6},{6,7},{7,0},{8,9},{9,10},{10,1... | collective-permute-start | bytes 393224 | tf_op jit(solution)/shard_map/ppermute | solution.py:455
  72.9 2.6 %collective-permute-done.8.r1n = f32[16,8,256]{2,1,0:T(8,128)S(1)} collective-permute-done((f32[16,8,256]{2,1,0:T(8,128)S(1)}, f32[16,8,256]{2,1,0:T(8,128)S(1)}, u32[]{:S(2)}, u32[]{:S(2)}) %collective-permute-start.8) | collective-permute-done | bytes 131104 | tf_op jit(solution)/shard_map/ppermute | solution.py:455
  75.5 0.0 collective-permute-done.7.r1p
  75.5 1.8 %middle_first.3 = (f32[16,16,256]{2,1,0:T(8,128)S(1)}, f32[18,16,256]{2,1,0:T(8,128)S(1)}, f32[128,128]{1,0:T(8,128)S(1)}) custom-call(f32[16,8,256]{2,1,0:T(8,128)S(1)} %collective-permute-done.7.r1p, f32[16,8,256]{2,1,0:T(8,128)S(1)} %get-tuple-element.55.r1, f32[16,8,256]{2,1,0:T(8,128)S(1)} %collective-permute-done.8.r1n, ...), custom_call_target="tpu_custom_call" | custom-call | bytes 1884160 | tf_op jit(solution)/shard_map/middle_first/pallas_call | solution.py:439
  77.4 11.4 %all_to_all.23 = f32[32,4,128]{2,1,0:T(4,128)S(1)} all-to-all(f32[32,4,128]{2,1,0:T(4,128)S(1)} %bitcast.9), channel_id=1, replica_groups=mesh['die'=4,'tile'=8] {'die','tile'}, dimensions={0} | all-to-all | bytes 131072 | tf_op jit(solution)/shard_map/all_to_all | solution.py:501
  88.8 10.0 %last.1 = (f32[2,4,16,512]{3,2,1,0:T(8,128)S(1)}, f32[2,4,16,512]{3,2,1,0:T(8,128)S(1)}, f32[2,4,16,512]{3,2,1,0:T(8,128)S(1)}, f32[2,4,16,512]{3,2,1,0:T(8,128)S(1)}) custom-call(s32[2]{0:T(128)S(1)} %pad_add_fusion.idx, f32[128,128]{1,0:T(8,128)S(1)} %bitcast.8, f32[16,8,128]{2,1,0:T(8,128)S(1)} %get-tuple-element.47.u2, ...), custom_call_target="tpu_custom_call" | custom-call | bytes 8765448 | tf_op jit(solution)/shard_map/last/pallas_call | solution.py:439
  98.8 0.1 collective-permute-start.9
  98.9 0.6 collective-permute-start.10
  99.5 2.0 %collective-permute-start.11 = (f32[2,4,16,512]{3,2,1,0:T(8,128)S(1)}, f32[2,4,16,512]{3,2,1,0:T(8,128)S(1)}, u32[]{:S(2)}, u32[]{:S(2)}) collective-permute-start(f32[2,4,16,512]{3,2,1,0:T(8,128)S(1)} %get-tuple-element.63), channel_id=1, source_target_pairs={{0,24},{8,0},{16,8},{24,16},{1,25},{9,1},{17,9},{25,17},{2,26},{10... | collective-permute-start | bytes 786440 | tf_op jit(solution)/shard_map/ppermute | solution.py:455
  101.5 5.8 %collective-permute-done.9.refs_1_ = f32[2,4,16,512]{3,2,1,0:T(8,128)S(1)} collective-permute-done((f32[2,4,16,512]{3,2,1,0:T(8,128)S(1)}, f32[2,4,16,512]{3,2,1,0:T(8,128)S(1)}, u32[]{:S(2)}, u32[]{:S(2)}) %collective-permute-start.9) | collective-permute-done | bytes 262176 | tf_op jit(solution)/shard_map/ppermute | solution.py:455
  107.3 4.7 %collective-permute-done.10.refs_2_ = f32[2,4,16,512]{3,2,1,0:T(8,128)S(1)} collective-permute-done((f32[2,4,16,512]{3,2,1,0:T(8,128)S(1)}, f32[2,4,16,512]{3,2,1,0:T(8,128)S(1)}, u32[]{:S(2)}, u32[]{:S(2)}) %collective-permute-start.10) | collective-permute-done | bytes 262176 | tf_op jit(solution)/shard_map/ppermute | solution.py:455
  112.0 0.0 collective-permute-done.11.refs_3_
  112.0 1.6 %unpack.1 = (f32[4,16,2048]{2,1,0:T(8,128)}, f32[4,16,2048]{2,1,0:T(8,128)}) custom-call(s32[2]{0:T(128)S(1)} %pad_add_fusion.idx, f32[2,4,16,512]{3,2,1,0:T(8,128)S(1)} %get-tuple-element.60.refs_0_, f32[2,4,16,512]{3,2,1,0:T(8,128)S(1)} %collective-permute-done.9.refs_1_, f32[2,4,16,512]{3,2,1,0:T(8,128)S(1)} %collective-permute-done.10.refs_2_, ...), custom_call_target="tpu_custom_call" | custom-call | bytes 2097160 | tf_op jit(solution)/shard_map/unpack/pallas_call | solution.py:439
Async XLA Ops:
  0.6 29.2 %copy-start = (bf16[640,256]{1,0:T(8,128)(2,1)S(1)}, bf16[640,256]{1,0:T(8,128)(2,1)}, u32[]{:S(2)}) copy-start(bf16[640,256]{1,0:T(8,128)(2,1)} %constant.16.clone.down) | copy-start | bytes 983044
  2.2 1.0 copy-start.3
  3.2 0.7 copy-start.5
  3.9 0.7 copy-start.6
  5.2 7.4 %collective-permute-start = (f32[72,640]{1,0:T(8,128)S(1)}, f32[72,640]{1,0:T(8,128)S(1)}, u32[]{:S(2)}, u32[]{:S(2)}) collective-permute-start(f32[72,640]{1,0:T(8,128)S(1)} %get-tuple-element.34), channel_id=1, source_target_pairs={{0,8},{8,16},{16,24},{24,0},{1,9},{9,17},{17,25},{25,1},{2,10},{10... | collective-permute-start | bytes 552968 | tf_op jit(solution)/shard_map/ppermute | solution.py:455
  7.2 10.0 %collective-permute-start.1 = (f32[72,640]{1,0:T(8,128)S(1)}, f32[72,640]{1,0:T(8,128)S(1)}, u32[]{:S(2)}, u32[]{:S(2)}) collective-permute-start(f32[72,640]{1,0:T(8,128)S(1)} %get-tuple-element.35), channel_id=1, source_target_pairs={{0,16},{8,24},{16,0},{24,8},{1,17},{9,25},{17,1},{25,9},{2,18},{10... | collective-permute-start | bytes 552968 | tf_op jit(solution)/shard_map/ppermute | solution.py:455
  8.5 8.8 %collective-permute-start.2 = (f32[72,640]{1,0:T(8,128)S(1)}, f32[72,640]{1,0:T(8,128)S(1)}, u32[]{:S(2)}, u32[]{:S(2)}) collective-permute-start(f32[72,640]{1,0:T(8,128)S(1)} %get-tuple-element.36), channel_id=1, source_target_pairs={{0,24},{8,0},{16,8},{24,16},{1,25},{9,1},{17,9},{25,17},{2,26},{10... | collective-permute-start | bytes 552968 | tf_op jit(solution)/shard_map/ppermute | solution.py:455
  17.9 7.0 %collective-permute-start.3 = (f32[16,8,640]{2,1,0:T(8,128)S(1)}, f32[16,8,640]{2,1,0:T(8,128)S(1)}, u32[]{:S(2)}, u32[]{:S(2)}) collective-permute-start(f32[16,8,640]{2,1,0:T(8,128)S(1)} %get-tuple-element.37.bot), channel_id=1, source_target_pairs={{0,1},{1,2},{2,3},{3,4},{4,5},{5,6},{6,7},{7,0},{8,9},{9,10},{10,1... | collective-permute-start | bytes 983048 | tf_op jit(solution)/shard_map/ppermute | solution.py:455
  19.9 9.9 %collective-permute-start.4 = (f32[16,8,640]{2,1,0:T(8,128)S(1)}, f32[16,8,640]{2,1,0:T(8,128)S(1)}, u32[]{:S(2)}, u32[]{:S(2)}) collective-permute-start(f32[16,8,640]{2,1,0:T(8,128)S(1)} %get-tuple-element.38.top), channel_id=1, source_target_pairs={{0,7},{1,0},{2,1},{3,2},{4,3},{5,4},{6,5},{7,6},{8,15},{9,8},{10,9... | collective-permute-start | bytes 983048 | tf_op jit(solution)/shard_map/ppermute | solution.py:455
  29.8 10.0 %copy-start.2 = (bf16[512,128]{1,0:T(8,128)(2,1)S(1)}, bf16[512,128]{1,0:T(8,128)(2,1)}, u32[]{:S(2)}) copy-start(bf16[512,128]{1,0:T(8,128)(2,1)} %constant.19.clone.down2) | copy-start | bytes 393220
  29.8 24.5 %copy-start.4 = (bf16[128,256]{1,0:T(8,128)(2,1)S(1)}, bf16[128,256]{1,0:T(8,128)(2,1)}, u32[]{:S(2)}) copy-start(bf16[128,256]{1,0:T(8,128)(2,1)} %constant.18.clone.spread2) | copy-start | bytes 196612
  34.9 19.4 %copy-start.1 = (bf16[256,640]{1,0:T(8,128)(2,1)S(1)}, bf16[256,640]{1,0:T(8,128)(2,1)}, u32[]{:S(2)}) copy-start(bf16[256,640]{1,0:T(8,128)(2,1)} %constant.17.clone.spread1) | copy-start | bytes 983044
  35.0 4.4 %collective-permute-start.6 = (f32[16,8,256]{2,1,0:T(8,128)S(1)}, f32[16,8,256]{2,1,0:T(8,128)S(1)}, u32[]{:S(2)}, u32[]{:S(2)}) collective-permute-start(f32[16,8,256]{2,1,0:T(8,128)S(1)} %get-tuple-element.43.r1), channel_id=1, source_target_pairs={{0,7},{1,0},{2,1},{3,2},{4,3},{5,4},{6,5},{7,6},{8,15},{9,8},{10,9... | collective-permute-start | bytes 393224 | tf_op jit(solution)/shard_map/ppermute | solution.py:455
  35.0 4.8 %collective-permute-start.5 = (f32[16,8,256]{2,1,0:T(8,128)S(1)}, f32[16,8,256]{2,1,0:T(8,128)S(1)}, u32[]{:S(2)}, u32[]{:S(2)}) collective-permute-start(f32[16,8,256]{2,1,0:T(8,128)S(1)} %get-tuple-element.43.r1), channel_id=1, source_target_pairs={{0,1},{1,2},{2,3},{3,4},{4,5},{5,6},{6,7},{7,0},{8,9},{9,10},{10,1... | collective-permute-start | bytes 393224 | tf_op jit(solution)/shard_map/ppermute | solution.py:455
  71.1 4.4 %collective-permute-start.8 = (f32[16,8,256]{2,1,0:T(8,128)S(1)}, f32[16,8,256]{2,1,0:T(8,128)S(1)}, u32[]{:S(2)}, u32[]{:S(2)}) collective-permute-start(f32[16,8,256]{2,1,0:T(8,128)S(1)} %get-tuple-element.55.r1), channel_id=1, source_target_pairs={{0,7},{1,0},{2,1},{3,2},{4,3},{5,4},{6,5},{7,6},{8,15},{9,8},{10,9... | collective-permute-start | bytes 393224 | tf_op jit(solution)/shard_map/ppermute | solution.py:455
  71.5 4.0 %collective-permute-start.7 = (f32[16,8,256]{2,1,0:T(8,128)S(1)}, f32[16,8,256]{2,1,0:T(8,128)S(1)}, u32[]{:S(2)}, u32[]{:S(2)}) collective-permute-start(f32[16,8,256]{2,1,0:T(8,128)S(1)} %get-tuple-element.55.r1), channel_id=1, source_target_pairs={{0,1},{1,2},{2,3},{3,4},{4,5},{5,6},{6,7},{7,0},{8,9},{9,10},{10,1... | collective-permute-start | bytes 393224 | tf_op jit(solution)/shard_map/ppermute | solution.py:455
  98.8 8.5 %collective-permute-start.9 = (f32[2,4,16,512]{3,2,1,0:T(8,128)S(1)}, f32[2,4,16,512]{3,2,1,0:T(8,128)S(1)}, u32[]{:S(2)}, u32[]{:S(2)}) collective-permute-start(f32[2,4,16,512]{3,2,1,0:T(8,128)S(1)} %get-tuple-element.61), channel_id=1, source_target_pairs={{0,8},{8,16},{16,24},{24,0},{1,9},{9,17},{17,25},{25,1},{2,10},{10... | collective-permute-start | bytes 786440 | tf_op jit(solution)/shard_map/ppermute | solution.py:455
  98.9 13.1 %collective-permute-start.10 = (f32[2,4,16,512]{3,2,1,0:T(8,128)S(1)}, f32[2,4,16,512]{3,2,1,0:T(8,128)S(1)}, u32[]{:S(2)}, u32[]{:S(2)}) collective-permute-start(f32[2,4,16,512]{3,2,1,0:T(8,128)S(1)} %get-tuple-element.62), channel_id=1, source_target_pairs={{0,16},{8,24},{16,0},{24,8},{1,17},{9,25},{17,1},{25,9},{2,18},{10... | collective-permute-start | bytes 786440 | tf_op jit(solution)/shard_map/ppermute | solution.py:455
  99.5 12.5 %collective-permute-start.11 = (f32[2,4,16,512]{3,2,1,0:T(8,128)S(1)}, f32[2,4,16,512]{3,2,1,0:T(8,128)S(1)}, u32[]{:S(2)}, u32[]{:S(2)}) collective-permute-start(f32[2,4,16,512]{3,2,1,0:T(8,128)S(1)} %get-tuple-element.63), channel_id=1, source_target_pairs={{0,24},{8,0},{16,8},{24,16},{1,25},{9,1},{17,9},{25,17},{2,26},{10... | collective-permute-start | bytes 786440 | tf_op jit(solution)/shard_map/ppermute | solution.py:455

commit v2 on v1

v2 whole, which is shorter than its diff:
```python
import functools

import jax
import jax.numpy as jnp
import numpy as np
from jax import lax
from jax.experimental import pallas as pl
from jax.experimental.pallas import tpu as pltpu
from jax.sharding import PartitionSpec as P

OMEGA = 0.8
NC = 6
LN = 128
HX = 64
HY = 8
F32 = jnp.float32
BF16 = jnp.bfloat16


def iota(shape, axis):
    return lax.broadcasted_iota(jnp.int32, shape, axis)


def split_dot(x, m):
    hi = x.astype(BF16)
    lo = (x - hi.astype(F32)).astype(BF16)
    return jnp.dot(hi, m, preferred_element_type=F32) + jnp.dot(lo, m, preferred_element_type=F32)


def pair_dot(a, b):
    return lax.dot_general(a, b, (((0,), (0,)), ((), ())), preferred_element_type=F32)


class Sizes:
    def __init__(self, mesh_shape, f_shape, n_blocks):
        self.nd, self.nt = mesh_shape["die"], mesh_shape["tile"]
        self.lz, self.rows, self.width = f_shape
        self.nb = n_blocks
        self.wc = self.width // self.nd
        self.we = self.wc + LN
        self.j0 = self.we // LN
        self.nz = self.nd * self.lz
        self.re = self.rows + 2 * HY
        self.own1 = self.rows // 4
        self.r1 = self.re // 4
        self.c1 = self.wc // 4
        self.e1 = 2 * self.r1
        self.pad1 = (self.e1 - self.own1) // 2
        self.j1 = 2
        self.w1 = self.j1 * LN
        self.c2 = self.wc // 16
        self.part = self.lz * self.j0 * self.rows
        assert self.rows == 16 and self.lz == 4 and self.c1 == LN
        assert self.nd * self.c2 == LN and self.nb <= LN and self.nt <= LN and self.nt % 8 == 0


def place():
    return lax.axis_index("die"), lax.axis_index("tile")


def tiles(j):
    return slice(j * LN, (j + 1) * LN)


def windows(lo, hi):
    return [min(r, hi - 8) for r in range(lo, hi, 8)]


def pack_kernel(s, mat_h, material_h, conductance_h, blocks_h, f_h, *refs):
    outs, (mat, material, conductance, blocks, f, sem) = refs[: s.nd], refs[s.nd :]
    pairs = [(f_h, f), (mat_h, mat), (material_h, material), (conductance_h, conductance), (blocks_h, blocks)]
    copies = [pltpu.make_async_copy(a, b, sem.at[k]) for k, (a, b) in enumerate(pairs)]
    for c in copies:
        c.start()
    for c in copies[1:]:
        c.wait()
    d, _ = place()
    lane, sub = iota((8, LN), 1), iota((8, LN), 0)
    info = jnp.where((sub == 5) & (lane == 0), conductance[0], 0.0)
    for z in range(s.lz):
        info = jnp.where((sub == 4) & (lane == z), mat[material[z]], info)
    for out in outs:
        out[s.part :, :] = info
        out[s.part : s.part + 4, : s.nb] = blocks[...].astype(F32)
    copies[0].wait()
    low = iota((s.rows, LN), 1) < HX
    for step, out in enumerate(outs):
        e = lax.rem(d + step, s.nd)
        right = lax.rem(e + 1, s.nd) * s.wc
        left = lax.rem(e + s.nd - 1, s.nd) * s.wc + (s.wc - LN)

        def column(z, at):
            return f[z, :, pl.ds(pl.multiple_of(at, LN), LN)]

        for z in range(s.lz):
            for j in range(s.j0):
                at = (z * s.j0 + j) * s.rows
                if j < s.j0 - 1:
                    x = column(z, e * s.wc + j * LN)
                else:
                    x = jnp.where(low, column(z, right), column(z, left))
                out[at : at + s.rows, :] = x


def assemble_kernel(s, *refs):
    parts, (top, bot, prm) = refs[: s.nd], refs[s.nd :]
    d, _ = place()
    n = s.lz * s.j0
    for step, part in enumerate(parts):
        e = lax.rem(d + s.nd - step, s.nd)
        for q in range(n):
            top[n * e + q] = part[q * s.rows : q * s.rows + HY, :]
            bot[n * e + q] = part[q * s.rows + HY : (q + 1) * s.rows, :]
        prm[e] = part[s.part :, :]


def overlap(lo, size, first, past):
    return jnp.maximum(jnp.minimum(lo + size, past) - jnp.maximum(lo, first), 0.0)


def coeff_kernel(s, prm, via0, d0, via1, d1, u2, l2, d2, c, u, c2):
    d, t = place()
    ny = s.rows * s.nt
    lane8, sub8 = iota((8, LN), 1), iota((8, LN), 0)

    def pick(tile, row, col):
        return jnp.sum(jnp.where((lane8 == col) & (sub8 == row), tile, 0.0), keepdims=True)

    info = [prm[g] for g in range(s.nd)]
    cond = [pick(info[z // s.lz], 4, z % s.lz) for z in range(s.nz)]
    via = [pick(info[g], 5, 0) for g in range(s.nd)]
    vert = [
        2.0 * cond[z] * cond[min(z + 1, s.nz - 1)] / (cond[z] + cond[min(z + 1, s.nz - 1)])
        for z in range(s.nz)
    ]
    blocks = []
    for g in range(s.nd):
        b = jnp.transpose(info[g])
        lane = iota((LN, 8), 1)
        col = [jnp.sum(jnp.where(lane == k, b, 0.0), axis=1, keepdims=True) for k in range(4)]
        col = [x[: s.nb] for x in col]
        blocks.append((col[0], col[0] + col[2], col[1], col[1] + col[3]))

    def columns(n, own, shape, axis):
        p = iota(shape, axis)
        return p, jnp.where(p >= n - own // 8, p - n, p)

    row0 = t * s.rows - HY + iota((1, LN), 1)
    row1 = t * s.own1 - s.pad1 + iota((1, LN), 1)
    _, col0 = columns(s.we, s.wc, (1, s.we), 1)
    _, col1 = columns(s.w1, s.c1, (1, s.w1), 1)
    col0 += d * s.wc
    col1 += d * s.c1
    via0[0] = jnp.zeros(via0.shape[1:], F32)
    via1[0] = jnp.zeros(via1.shape[1:], F32)
    for g in range(s.nd):
        r0, r1, c0, c1 = blocks[g]
        a = overlap(row0.astype(F32), 1.0, r0, r1).astype(BF16)
        b = overlap(col0.astype(F32), 1.0, c0, c1).astype(BF16)
        m = pair_dot(a, b)[: s.re] * via[g]
        for j in range(s.j0):
            via0[g + 1, j] = m[:, tiles(j)]
        a = overlap(row1.astype(F32) * 4.0, 4.0, r0, r1).astype(BF16)
        b = overlap(col1.astype(F32) * 4.0, 4.0, c0, c1).astype(BF16)
        m = pair_dot(a, b)[: s.e1] * via[g]
        for j in range(s.j1):
            via1[g + 1, j] = m[:, tiles(j)]
    for z in range(s.nz):
        c[z] = jnp.zeros((8, LN), F32) + cond[z]
        u[z] = jnp.zeros((8, LN), F32) + vert[z]

    rr = t * s.rows - HY + iota((s.re, s.we), 0)
    _, cc = columns(s.we, s.wc, (s.re, s.we), 1)
    cc += d * s.wc
    in0 = jnp.where((rr >= 0) & (rr < ny) & (cc >= 0) & (cc < s.width), OMEGA, 0.0)
    rr = t * s.own1 - s.pad1 + iota((s.e1, s.w1), 0)
    pp, cc = columns(s.w1, s.c1, (s.e1, s.w1), 1)
    cc += d * s.c1
    in1 = (rr >= 0) & (rr < ny // 4) & (cc >= 0) & (cc < s.width // 4)
    in1 = jnp.where(in1 & ((pp < s.c1 + HX // 4) | (pp >= s.w1 - HX // 4)), OMEGA, 0.0)
    for level, (inside, nj, vp, out) in enumerate(((in0, s.j0, via0, d0), (in1, s.j1, via1, d1))):
        for z in range(s.nz):
            g, a = z // s.lz, z % s.lz
            const = 4.0 * cond[z] * 4.0**level
            if a < s.lz - 1:
                const = const + vert[z] * 16.0**level
            if a > 0:
                const = const + vert[z - 1] * 16.0**level
            for j in range(nj):
                diag = const
                if a == s.lz - 1:
                    diag = diag + vp[g + 1, j]
                if a == 0:
                    diag = diag + vp[g, j]
                out[z, j] = inside[:, tiles(j)] / diag

    group = iota((1, LN), 1) // s.c2
    xin = iota((1, LN), 1) % s.c2

    def by_group(values):
        out = jnp.zeros((1, LN), F32)
        for g in range(s.nd):
            out = jnp.where(group == g, values[g], out)
        return out

    cl = [by_group([cond[s.lz * g + a] for g in range(s.nd)]) * 16.0 for a in range(s.lz)]
    vl = [by_group([vert[s.lz * g + a] for g in range(s.nd)]) * 256.0 for a in range(s.lz)]
    vial = by_group(via)
    row2 = (iota((1, LN), 1) * 16).astype(F32)
    ra = jnp.concatenate([overlap(row2, 16.0, b[0], b[1]) for b in blocks], axis=0).astype(BF16)
    zero2 = jnp.zeros((s.nt, LN), F32)
    for a in range(s.lz):
        c2[a] = jnp.zeros((8, LN), F32) + cl[a]
    for e in range(s.nd):
        col2 = ((e * s.c2 + xin) * 16).astype(F32)
        cb = jnp.concatenate(
            [jnp.where(group == g, overlap(col2, 16.0, b[2], b[3]), 0.0) for g, b in enumerate(blocks)],
            axis=0,
        ).astype(BF16)
        v2 = pair_dot(ra, cb)[: s.nt] * vial
        ups = [zero2 + vl[a] for a in range(s.lz - 1)] + [v2]
        first = jnp.where(iota((s.nt, LN), 1) >= s.c2, pltpu.roll(v2, s.c2, 1), 0.0)
        lows = [first] + ups[:-1]
        for a in range(s.lz):
            q = e * s.lz + a
            u2[q] = ups[a]
            l2[q] = lows[a]
            d2[q] = OMEGA / (4.0 * cl[a] + ups[a] + lows[a])


class Level:
    def __init__(self, s, level, via, inv, c, u):
        self.s, self.via, self.inv, self.c, self.u = s, via, inv, c, u
        self.nj = (s.j0, s.j1)[level]
        self.cs, self.us = 4.0**level, 16.0**level

    def layers(self, body):
        s = self.s

        def group(g, carry):
            for a in range(s.lz):
                z = g * s.lz + a
                if a < s.lz - 1:
                    const_up = self.u[z] * self.us
                    up = lambda j, rows, k=const_up: k
                else:
                    up = lambda j, rows: self.via[g + 1, j, rows, :]
                if a > 0:
                    const_down = self.u[z - 1] * self.us
                    down = lambda j, rows, k=const_down: k
                else:
                    down = lambda j, rows: self.via[g, j, rows, :]
                body(z, self.c[z] * self.cs, up, down)
            return carry

        lax.fori_loop(0, s.nd, group, 0)

    def off_diagonal(self, src, z, r, c, up, down, count=None):
        n = self.nj
        lane = iota((8, LN), 1)
        first, last = lane == 0, lane == LN - 1
        rows = pl.ds(r, 8)
        v = [src[z + 1, j, rows, :] for j in range(n)]
        ahead = [pltpu.roll(x, LN - 1, 1) for x in v]
        behind = [pltpu.roll(x, 1, 1) for x in v]
        out = []
        for j in range(n if count is None else count):
            x = jnp.where(last, ahead[(j + 1) % n], ahead[j]) + jnp.where(first, behind[j - 1], behind[j])
            y = src[z + 1, j, pl.ds(r - 1, 8), :] + src[z + 1, j, pl.ds(r + 1, 8), :]
            k_up, k_down = up(j, rows), down(j, rows)
            g = c * (x + y) + (k_up * src[z + 2, j, rows, :] + k_down * src[z, j, rows, :])
            out.append((j, v[j], g, k_up, k_down))
        return out

    def sweep(self, src, dst, f, lo, hi):
        def body(z, c, up, down):
            for r in windows(lo, hi):
                rows = pl.ds(r, 8)
                for j, v, g, _, _ in self.off_diagonal(src, z, r, c, up, down):
                    dst[z + 1, j, rows, :] = (1.0 - OMEGA) * v + self.inv[z, j, rows, :] * (f[z, j, rows, :] + g)

        self.layers(body)

    def residual(self, src, f, lo, hi, put, count=None):
        def body(z, c, up, down):
            four = 4.0 * c
            for r in windows(lo, hi):
                for j, v, g, k_up, k_down in self.off_diagonal(src, z, r, c, up, down, count):
                    put(z, j, r, (f[z, j, pl.ds(r, 8), :] + g) - (four + k_up + k_down) * v)

        self.layers(body)


def zero_ends(s, *bufs):
    for b in bufs:
        b[0] = jnp.zeros(b.shape[1:], F32)
        b[s.nz + 1] = jnp.zeros(b.shape[1:], F32)


def restrict(s, level, src, f, lo, hi, down, rbuf, sums, r1):
    n = s.nz * s.j0 * s.re
    for k in range(0, s.nz * s.j0):
        if lo > 0:
            rbuf[k * s.re : k * s.re + lo, :] = jnp.zeros((lo, LN), F32)
            rbuf[k * s.re + hi : (k + 1) * s.re, :] = jnp.zeros((s.re - hi, LN), F32)

    def put(z, j, r, x):
        rbuf[pl.ds((z * s.j0 + j) * s.re + r, 8), :] = x

    level.residual(src, f, lo, hi, put)

    def body(z, carry):
        for j in range(s.j0):
            part = [rbuf[pl.ds((z * s.j0 + j) * s.re + k, s.r1, stride=4), :] for k in range(4)]
            sums[z, :, tiles(j)] = (part[0] + part[1]) + (part[2] + part[3])
        return carry

    lax.fori_loop(0, s.nz, body, 0)
    out = split_dot(sums[...].reshape(s.nz * s.r1, s.we), down[...])
    for z in range(s.nz):
        for j in range(s.j1):
            r1[z, j] = out[z * s.r1 : (z + 1) * s.r1, tiles(j)]


def fine_first_kernel(s, above, top, bot, below, via0, d0, c, u, down, f, v2, r1, va, rbuf, sums):
    level = Level(s, 0, via0, d0, c, u)
    zero_ends(s, va, v2)

    def body(z, carry):
        for j in range(s.j0):
            for k, ref in enumerate((above, top, bot, below)):
                rows = slice(k * HY, (k + 1) * HY)
                x = ref[z * s.j0 + j]
                f[z, j, rows, :] = x
                va[z + 1, j, rows, :] = d0[z, j, rows, :] * x
        return carry

    lax.fori_loop(0, s.nz, body, 0)
    level.sweep(va, v2, f, 1, s.re - 1)
    restrict(s, level, v2, f, HY - 4, s.re - HY + 4, down, rbuf, sums, r1)


def middle_first_kernel(s, r1p, r1, r1n, via1, d1, c, u, down2, rx, w2, send, wa, buf):
    level = Level(s, 1, via1, d1, c, u)
    half, own, pad = s.r1, s.own1, s.pad1
    sub = iota((half, LN), 0)
    zero_ends(s, wa, w2)

    def body(z, carry):
        for j in range(s.j1):
            mid = pltpu.roll(r1[z, j], half // 2, 0)
            up = jnp.where(sub >= pad, mid, r1p[z, j])
            down = jnp.where(sub < own - (half - pad), mid, r1n[z, j])
            rx[z, j, :half, :] = up
            rx[z, j, half:, :] = down
            wa[z + 1, j, :half, :] = d1[z, j, :half, :] * up
            wa[z + 1, j, half:, :] = d1[z, j, half:, :] * down
        return carry

    lax.fori_loop(0, s.nz, body, 0)
    level.sweep(wa, w2, rx, pad - 4, pad + own + 4)

    def put(z, j, r, x):
        buf[pl.ds(pl.multiple_of(z * 8, 8), 8), :] = x

    level.residual(w2, rx, pad - 2, pad + own + 2, put, 1)
    sub8, group = iota((8, LN), 0), iota((8, LN), 1) // s.c2
    tile = jnp.zeros((8, LN), F32)
    for h in range(s.nz // 8):
        part = [buf[pl.ds(64 * h + 2 + k, 8, stride=8), :] for k in range(own)]
        x = split_dot((part[0] + part[1]) + (part[2] + part[3]), down2[...])
        y = pltpu.roll(x, 4, 0)
        for g in (2 * h, 2 * h + 1):
            tile = jnp.where(group == g, jnp.where((sub8 < 4) == (g % 2 == 0), x, y), tile)
    for k in range(s.nd * s.nt * s.lz // 8):
        send[8 * k : 8 * k + 8, :] = tile


def coarse(s, got, u2, l2, d2, c2, cs):
    lane = iota((s.nt, LN), 1)
    x, t = lane % s.c2, iota((s.nt, LN), 0)
    first_x, last_x = x == 0, x == s.c2 - 1
    slabs = s.nd * s.lz
    rhs, v = [], []
    for q in range(slabs):
        e, a = q // s.lz, q % s.lz
        r = got[pl.ds(e * s.nt * s.lz + a, s.nt, stride=s.lz), :]
        rhs.append(r)
        v.append(d2[q] * r)
    zero = jnp.zeros((s.nt, LN), F32)

    def body(_, v):
        new = []
        for q in range(slabs):
            e, a = q // s.lz, q % s.lz
            w = v[q]
            right = pltpu.roll(v[q + s.lz], s.c2 - 1, 1) if e < s.nd - 1 else zero
            left = pltpu.roll(v[q - s.lz], LN - (s.c2 - 1), 1) if e > 0 else zero
            side = jnp.where(last_x, right, pltpu.roll(w, LN - 1, 1))
            side += jnp.where(first_x, left, pltpu.roll(w, 1, 1))
            side += jnp.where(t == s.nt - 1, 0.0, pltpu.roll(w, s.nt - 1, 0))
            side += jnp.where(t == 0, 0.0, pltpu.roll(w, 1, 0))
            if a < s.lz - 1:
                up = v[q + 1]
            else:
                up = jnp.where(lane >= LN - s.c2, 0.0, pltpu.roll(v[q - a], LN - s.c2, 1))
            if a > 0:
                down = v[q - 1]
            else:
                down = jnp.where(lane < s.c2, 0.0, pltpu.roll(v[q + s.lz - 1], s.c2, 1))
            g = c2[a, 0:1, :] * side + u2[q] * up + l2[q] * down
            new.append((1.0 - OMEGA) * w + d2[q] * (rhs[q] + g))
        return tuple(new)

    v = lax.fori_loop(0, NC - 1, body, tuple(v))
    for q in range(slabs):
        cs[q, :HY, :] = jnp.zeros((HY, LN), F32)
        cs[q, HY + s.nt :, :] = jnp.zeros((HY, LN), F32)
        cs[q, HY : HY + s.nt, :] = v[q]


def middle_last(s, level, cs, spread2, w2, rx, comp, wide, wa, wb):
    d, t = place()
    lane, upper = iota((8, LN), 1), iota((8, LN), 0) < 4
    after = lax.rem(d + 1, s.nd) * s.lz
    before = lax.rem(d + s.nd - 1, s.nd) * s.lz
    zero_ends(s, wa, wb)
    for a in range(s.lz):
        rows = [cs[base + a, pl.ds(HY - 1 + t, 8), :] for base in (d * s.lz, after, before)]
        for g in range(s.nd):
            turn = []
            for r, by in zip(rows, (0, s.c2, LN - s.c2)):
                by = (by - g * s.c2) % LN
                turn.append(pltpu.roll(r, by, 1) if by else r)
            z = g * s.lz + a
            comp[8 * z : 8 * z + 8, :] = jnp.where(
                lane < s.c2, turn[0], jnp.where(lane < LN // 2, turn[1], turn[2])
            )
    wide[...] = split_dot(comp[...], spread2[...]).reshape(wide.shape)

    def body(z, carry):
        for j in range(s.j1):
            x = [wide[z, k : k + 1, tiles(j)] for k in range(3)]
            for k in range(2):
                rows = slice(s.pad1 - 4 + 4 * k, s.pad1 + 4 + 4 * k)
                y = w2[z + 1, j, rows, :] + jnp.where(upper, x[k], x[k + 1])
                wa[z + 1, j, rows, :] = jnp.where(level.inv[z, j, rows, :] > 0.0, y, 0.0)
        return carry

    lax.fori_loop(0, s.nz, body, 0)
    level.sweep(wa, wb, rx, s.pad1 - 3, s.pad1 + s.own1 + 3)
    level.sweep(wb, wa, rx, s.pad1 - 2, s.pad1 + s.own1 + 2)


def correct_fine(s, w, v, spread1, wide, dst):
    rows = slice(s.pad1 - 2, s.pad1 + s.own1 + 2)
    lhs = jnp.concatenate([w[1 : s.nz + 1, j, rows, :].reshape(s.nz * s.r1, LN) for j in range(s.j1)], axis=1)
    wide[...] = split_dot(lhs, spread1[...]).reshape(wide.shape)
    zero_ends(s, dst)
    upper = iota((8, LN), 0) < 4

    def body(z, carry):
        for j in range(s.j0):
            for k in range(s.r1 // 2):
                rows = slice(8 * k, 8 * k + 8)
                x = [wide[z, 2 * k + i : 2 * k + i + 1, tiles(j)] for i in range(2)]
                dst[z + 1, j, rows, :] = v[z + 1, j, rows, :] + jnp.where(upper, x[0], x[1])
        return carry

    lax.fori_loop(0, s.nz, body, 0)


def back_kernel(
    s, got, u2, l2, d2, c2, w2, rx, via1, d1, c, u, v2, f, via0, d0, spread2, spread1, down,
    v, r1, cs, comp, wide2, wa, wb, va, wide, rbuf,
):
    fine, middle = Level(s, 0, via0, d0, c, u), Level(s, 1, via1, d1, c, u)
    coarse(s, got, u2, l2, d2, c2, cs)
    middle_last(s, middle, cs, spread2, w2, rx, comp, wide2, wa, wb)
    correct_fine(s, wa, v2, spread1, wide, va)
    zero_ends(s, v)
    fine.sweep(va, v, f, 2, s.re - 2)
    fine.sweep(v, va, f, 3, s.re - 3)
    fine.sweep(va, v, f, 4, s.re - 4)
    fine.sweep(v, va, f, 5, s.re - 5)
    restrict(s, fine, va, f, HY, HY + s.rows, down, rbuf, wide, r1)

    def body(z, carry):
        for j in range(s.j0):
            for r in windows(5, s.re - 5):
                v[z + 1, j, r : r + 8, :] = va[z + 1, j, r : r + 8, :]
        return carry

    lax.fori_loop(0, s.nz, body, 0)


def last_kernel(
    s, got, u2, l2, d2, c2, w2, rx, via1, d1, c, u, v2, f, via0, d0, spread2, spread1, *refs,
):
    outs, (cs, comp, wide2, wa, wb, va, wide, vb, rbuf) = refs[: s.nd], refs[s.nd :]
    fine, middle = Level(s, 0, via0, d0, c, u), Level(s, 1, via1, d1, c, u)
    d, _ = place()
    coarse(s, got, u2, l2, d2, c2, cs)
    middle_last(s, middle, cs, spread2, w2, rx, comp, wide2, wa, wb)
    correct_fine(s, wa, v2, spread1, wide, va)
    zero_ends(s, vb)
    fine.sweep(va, vb, f, HY - 2, HY + s.rows + 2)
    fine.sweep(vb, va, f, HY - 1, HY + s.rows + 1)

    def put(z, j, r, x):
        rbuf[pl.ds(pl.multiple_of((z * (s.j0 - 1) + j) * s.rows + (r - HY), 8), 8), :] = x

    fine.residual(va, f, HY, HY + s.rows, put, s.j0 - 1)
    for step, out in enumerate(outs):
        e = lax.rem(d + step, s.nd)
        for a in range(s.lz):
            z = e * s.lz + a
            for j in range(s.j0 - 1):
                out[0, a, :, tiles(j)] = va[z + 1, j, HY : HY + s.rows, :]
                at = pl.multiple_of((z * (s.j0 - 1) + j) * s.rows, 8)
                out[1, a, :, tiles(j)] = rbuf[pl.ds(at, s.rows), :]


def unpack_kernel(s, *refs):
    parts, outs, sem = refs[: s.nd], refs[s.nd : -1], refs[-1]
    d, _ = place()
    copies = []
    for step, part in enumerate(parts):
        e = lax.rem(d + s.nd - step, s.nd)
        cols = pl.ds(pl.multiple_of(e * s.wc, LN), s.wc)
        for k, out in enumerate(outs):
            copies.append(pltpu.make_async_copy(part.at[k], out.at[:, :, cols], sem.at[len(outs) * step + k]))
    for c in copies:
        c.start()
    for c in copies:
        c.wait()


def call(name, kernel, s, outs, scratch=(), host_in=False, host_out=False):
    shapes = [jax.ShapeDtypeStruct(o, F32) for o in outs]
    spaces = [pl.BlockSpec(memory_space=m) for m in (pltpu.VMEM, pltpu.HBM)]

    def run(*args):
        total = sum(int(np.prod(a.shape)) * 4 for a in args) + sum(int(np.prod(o)) * 4 for o in outs)
        return pl.pallas_call(
            functools.partial(kernel, s),
            name=name,
            out_shape=shapes,
            in_specs=[spaces[host_in]] * len(args),
            out_specs=[spaces[host_out]] * len(outs),
            scratch_shapes=[pltpu.VMEM(x, F32) if isinstance(x, tuple) else x for x in scratch],
            compiler_params=pltpu.CompilerParams(vmem_limit_bytes=32 << 20),
            cost_estimate=pl.CostEstimate(flops=4 * total, bytes_accessed=total, transcendentals=0),
        )(*args)

    return run


def shift(x, axis, by):
    n = lax.axis_size(axis)
    return lax.ppermute(x, axis, [(i, (i + by) % n) for i in range(n)])


def tables(s):
    p = np.arange(s.we)
    at = p // 4 + np.where(p >= s.wc + HX, s.w1 - s.we // 4, 0)
    down = at[:, None] == np.arange(s.w1)[None, :]
    q = np.arange(s.w1)
    k = q // 4 + np.where(q >= s.w1 - HX // 4, LN - s.w1 // 4, 0)
    used = (q < s.c1 + HX // 4) | (q >= s.w1 - HX // 4)
    spread2 = (np.arange(LN)[:, None] == k[None, :]) & used[None, :]
    r = np.arange(LN)
    down2 = (r // 4)[:, None] == (r % s.c2)[None, :]
    return [jnp.asarray(m, BF16) for m in (down, down.T, spread2, down2)]


def local(s, source_heating, material_thermal_values, layer_material, via_conductance, via_blocks):
    down, spread1, spread2, down2 = tables(s)
    dma, smem = pltpu.SemaphoreType.DMA, pltpu.SMEM
    packed = (s.part + 8, LN)
    sends = call(
        "pack", pack_kernel, s, [packed] * s.nd,
        [
            smem(material_thermal_values.shape, F32), smem(layer_material.shape, jnp.int32),
            smem(via_conductance.shape, F32), pltpu.VMEM((4, s.nb), jnp.int32),
            pltpu.VMEM(source_heating.shape, F32), dma((5,)),
        ],
        host_in=True,
    )(material_thermal_values, layer_material, via_conductance, via_blocks[0].T, source_heating)
    parts = [sends[0]] + [shift(sends[k], "die", k) for k in range(1, s.nd)]
    half = (s.nz * s.j0, HY, LN)
    top, bot, prm = call("assemble", assemble_kernel, s, [half, half, (s.nd, 8, LN)])(*parts)
    above, below = shift(bot, "tile", 1), shift(top, "tile", -1)
    f0, f1, small = (s.j0, s.re, LN), (s.j1, s.e1, LN), (s.nz, s.j1, s.r1, LN)
    fine, fine_v = (s.nz, *f0), (s.nz + 2, *f0)
    mid, mid_v = (s.nz, *f1), (s.nz + 2, *f1)
    slab = (s.nd * s.lz, s.nt, LN)
    via0, d0, via1, d1, u2, l2, d2, c, u, c2 = call(
        "coeff", coeff_kernel, s,
        [(s.nd + 1, *f0), fine, (s.nd + 1, *f1), mid, slab, slab, slab, (s.nz, 8, LN), (s.nz, 8, LN), (s.lz, 8, LN)],
    )(prm)
    flat, rbuf = (s.nz, s.r1, s.we), (s.nz * s.j0 * s.re, LN)
    f, v, r1 = call("fine_first", fine_first_kernel, s, [fine, fine_v, small], [fine_v, rbuf, flat])(
        above, top, bot, below, via0, d0, c, u, down
    )
    spaces = [(s.nd * s.lz, s.nt + 2 * HY, LN), (s.nz * 8, LN), (s.nz, 8, s.w1), mid_v, mid_v, fine_v, flat]
    for cycle in range(2):
        rx, w2, send = call(
            "middle_first", middle_first_kernel, s,
            [mid, mid_v, (s.nd * s.nt * s.lz, LN)], [mid_v, (s.nz * 8, LN)],
        )(shift(r1, "tile", 1), r1, shift(r1, "tile", -1), via1, d1, c, u, down2)
        got = lax.all_to_all(send, ("die", "tile"), 0, 0, tiled=True)
        args = (got, u2, l2, d2, c2, w2, rx, via1, d1, c, u, v, f, via0, d0, spread2, spread1)
        if cycle == 0:
            v, r1 = call("back", back_kernel, s, [fine_v, small], spaces + [rbuf])(*args, down)
    piece = (2, s.lz, s.rows, s.wc)
    sends = call(
        "last", last_kernel, s, [piece] * s.nd, spaces + [fine_v, (s.nz * (s.j0 - 1) * s.rows, LN)]
    )(*args)
    parts = [sends[0]] + [shift(sends[k], "die", k) for k in range(1, s.nd)]
    whole = (s.lz, s.rows, s.width)
    return tuple(call("unpack", unpack_kernel, s, [whole] * 2, [dma((2 * s.nd,))], host_out=True)(*parts))


def solution(mesh):
    in_specs = (P("die", "tile", None), P(), P("die"), P("die"), P("die", None, None))
    out_specs = (P("die", "tile", None), P("die", "tile", None))

    def body(f, mat, material, conductance, blocks):
        s = Sizes(mesh.shape, f.shape, blocks.shape[1])
        return local(s, f, mat, material, conductance, blocks)

    return jax.shard_map(body, mesh=mesh, in_specs=in_specs, out_specs=out_specs, check_vma=False)
```

time: 115 us -> 95.2 us (0.83)
  Pallas kernels: 39.8 us -> 20.4 us
    pallas_call x9, Pallas kernels: 39.8 us -> 20.4 us  [run(): pl.pallas_call(functools.partial(kernel, s), name=name, out_shape=shapes,...]
    unnamed x14 -> x16, local copies, waits for them, and re-layouts: 2.37 us -> 3.04 us
where the time goes in v2:
time: 95.2 us; the launch traced here: 93.7 us
  waiting for transfers between devices  32 us (34%)
  blocking collectives  24 us (25%)
  Pallas kernels  20.4 us (21%)
  starting transfers between devices  12.7 us (13%)
  local copies, waits for them, and re-layouts  3.04 us (3%)
  between operations  1.41 us (1%)
    ppermute x12, waiting for transfers between devices, shift(): return lax.ppermute(x, axis, [(i, (i + by) % n) for i in range(n)])  32 us
    all_to_all x2, blocking collectives, local(): got = lax.all_to_all(send, ('die', 'tile'), 0, 0, tiled=True)  24 us
    pallas_call x9, Pallas kernels, run(): pl.pallas_call(functools.partial(kernel, s), name=name, out_shape=shapes,...  20.4 us
    ppermute x12, starting transfers between devices, shift(): return lax.ppermute(x, axis, [(i, (i + by) % n) for i in range(n)])  12.7 us
    unnamed x16, local copies, waits for them, and re-layouts  3.04 us
  transfers between devices with their start and end apart: 12, of which 9 were waited for; matrix products, arithmetic and copies ran while one was open for 0% of the time, Pallas kernels for 1%

profile of v2, /device:TPU:1, one launch (start us, length us, event | category | flops | bytes accessed | tf_op | source)
XLA Modules:
  0.0 93.7 jit_solution(3660492305719561231)
XLA Ops:
  0.6 0.0 copy-start.1
  1.3 0.0 copy-start.2
  1.3 1.0 %copy-done.2 = f32[4,16,2048]{2,1,0:T(8,128)S(1)} copy-done((f32[4,16,2048]{2,1,0:T(8,128)S(1)}, f32[4,16,2048]{2,1,0:T(8,128)}, u32[]{:S(2)}) %copy-start.2) | copy-done | bytes 524312
  2.4 0.0 copy-start.5
  2.4 0.7 copy-done.5
  3.1 0.0 copy-start.6
  3.1 0.7 copy-done.6
  3.7 0.0 copy-start.7
  3.7 0.7 copy-done.7
  4.4 0.8 pack.1
  5.1 2.1 %collective-permute-start = (f32[328,128]{1,0:T(8,128)S(1)}, f32[328,128]{1,0:T(8,128)S(1)}, u32[]{:S(2)}, u32[]{:S(2)}) collective-permute-start(f32[328,128]{1,0:T(8,128)S(1)} %get-tuple-element.35), channel_id=1, source_target_pairs={{0,8},{8,16},{16,24},{24,0},{1,9},{9,17},{17,25},{25,1},{2,10},{10... | collective-permute-start | bytes 503816 | tf_op jit(solution)/shard_map/ppermute | solution.py:561
  7.2 1.2 %collective-permute-start.1 = (f32[328,128]{1,0:T(8,128)S(1)}, f32[328,128]{1,0:T(8,128)S(1)}, u32[]{:S(2)}, u32[]{:S(2)}) collective-permute-start(f32[328,128]{1,0:T(8,128)S(1)} %get-tuple-element.36), channel_id=1, source_target_pairs={{0,16},{8,24},{16,0},{24,8},{1,17},{9,25},{17,1},{25,9},{2,18},{10... | collective-permute-start | bytes 503816 | tf_op jit(solution)/shard_map/ppermute | solution.py:561
  8.5 1.2 %collective-permute-start.2 = (f32[328,128]{1,0:T(8,128)S(1)}, f32[328,128]{1,0:T(8,128)S(1)}, u32[]{:S(2)}, u32[]{:S(2)}) collective-permute-start(f32[328,128]{1,0:T(8,128)S(1)} %get-tuple-element.37), channel_id=1, source_target_pairs={{0,24},{8,0},{16,8},{24,16},{1,25},{9,1},{17,9},{25,17},{2,26},{10... | collective-permute-start | bytes 503816 | tf_op jit(solution)/shard_map/ppermute | solution.py:561
  9.6 2.6 %collective-permute-done.refs_1_ = f32[328,128]{1,0:T(8,128)S(1)} collective-permute-done((f32[328,128]{1,0:T(8,128)S(1)}, f32[328,128]{1,0:T(8,128)S(1)}, u32[]{:S(2)}, u32[]{:S(2)}) %collective-permute-start) | collective-permute-done | bytes 167968 | tf_op jit(solution)/shard_map/ppermute | solution.py:561
  12.2 4.3 %collective-permute-done.1.refs_2_ = f32[328,128]{1,0:T(8,128)S(1)} collective-permute-done((f32[328,128]{1,0:T(8,128)S(1)}, f32[328,128]{1,0:T(8,128)S(1)}, u32[]{:S(2)}, u32[]{:S(2)}) %collective-permute-start.1) | collective-permute-done | bytes 167968 | tf_op jit(solution)/shard_map/ppermute | solution.py:561
  16.5 0.0 collective-permute-done.2.refs_3_
  16.5 0.1 assemble.1
  16.6 2.0 %collective-permute-start.3 = (f32[80,8,128]{2,1,0:T(8,128)S(1)}, f32[80,8,128]{2,1,0:T(8,128)S(1)}, u32[]{:S(2)}, u32[]{:S(2)}) collective-permute-start(f32[80,8,128]{2,1,0:T(8,128)S(1)} %get-tuple-element.38.bot), channel_id=1, source_target_pairs={{0,1},{1,2},{2,3},{3,4},{4,5},{5,6},{6,7},{7,0},{8,9},{9,10},{10,1... | collective-permute-start | bytes 983048 | tf_op jit(solution)/shard_map/ppermute | solution.py:561
  18.6 0.0 collective-permute-start.4
  18.6 1.0 %coeff.1 = (f32[5,5,32,128]{3,2,1,0:T(8,128)S(1)}, f32[16,5,32,128]{3,2,1,0:T(8,128)S(1)}, f32[5,2,16,128]{3,2,1,0:T(8,128)S(1)}, f32[16,2,16,128]{3,2,1,0:T(8,1...) custom-call(f32[4,8,128]{2,1,0:T(8,128)S(1)} %get-tuple-element.40.prm), custom_call_target="tpu_custom_call" | custom-call | flops 9699328 | bytes 2424832 | tf_op jit(solution)/shard_map/coeff/pallas_call | solution.py:545
  19.6 4.0 %collective-permute-done.3.above = f32[80,8,128]{2,1,0:T(8,128)S(1)} collective-permute-done((f32[80,8,128]{2,1,0:T(8,128)S(1)}, f32[80,8,128]{2,1,0:T(8,128)S(1)}, u32[]{:S(2)}, u32[]{:S(2)}) %collective-permute-start.3) | collective-permute-done | bytes 327712 | tf_op jit(solution)/shard_map/ppermute | solution.py:561
  23.6 5.0 %collective-permute-done.4.below = f32[80,8,128]{2,1,0:T(8,128)S(1)} collective-permute-done((f32[80,8,128]{2,1,0:T(8,128)S(1)}, f32[80,8,128]{2,1,0:T(8,128)S(1)}, u32[]{:S(2)}, u32[]{:S(2)}) %collective-permute-start.4) | collective-permute-done | bytes 327712 | tf_op jit(solution)/shard_map/ppermute | solution.py:561
  28.5 0.0 copy-done.1
  28.5 0.0 copy-start.4
  28.6 0.0 copy-start
  28.6 0.0 copy-start.3
  28.6 2.6 %fine_first.1 = (f32[16,5,32,128]{3,2,1,0:T(8,128)S(1)}, f32[18,5,32,128]{3,2,1,0:T(8,128)S(1)}, f32[16,2,8,128]{3,2,1,0:T(8,128)S(1)}) custom-call(f32[80,8,128]{2,1,0:T(8,128)S(1)} %collective-permute-done.3.above, f32[80,8,128]{2,1,0:T(8,128)S(1)} %get-tuple-element.39.top, f32[80,8,128]{2,1,0:T(8,128)S(1)} %get-tuple-element.38.bot, ...), custom_call_target="tpu_custom_call" | custom-call | flops 26935296 | bytes 6733824 | tf_op jit(solution)/shard_map/fine_first/pallas_call | solution.py:545
  31.2 0.1 collective-permute-start.6
  31.2 1.7 %collective-permute-start.5 = (f32[16,2,8,128]{3,2,1,0:T(8,128)S(1)}, f32[16,2,8,128]{3,2,1,0:T(8,128)S(1)}, u32[]{:S(2)}, u32[]{:S(2)}) collective-permute-start(f32[16,2,8,128]{3,2,1,0:T(8,128)S(1)} %get-tuple-element.45.r1), channel_id=1, source_target_pairs={{0,1},{1,2},{2,3},{3,4},{4,5},{5,6},{6,7},{7,0},{8,9},{9,10},{10,1... | collective-permute-start | bytes 393224 | tf_op jit(solution)/shard_map/ppermute | solution.py:561
  33.0 2.6 %collective-permute-done.6.r1n = f32[16,2,8,128]{3,2,1,0:T(8,128)S(1)} collective-permute-done((f32[16,2,8,128]{3,2,1,0:T(8,128)S(1)}, f32[16,2,8,128]{3,2,1,0:T(8,128)S(1)}, u32[]{:S(2)}, u32[]{:S(2)}) %collective-permute-start.6) | collective-permute-done | bytes 131104 | tf_op jit(solution)/shard_map/ppermute | solution.py:561
  35.6 0.4 collective-permute-done.5.r1p
  36.0 0.0 copy-done.4
  36.0 1.1 %middle_first.2 = (f32[16,2,16,128]{3,2,1,0:T(8,128)S(1)}, f32[18,2,16,128]{3,2,1,0:T(8,128)S(1)}, f32[128,128]{1,0:T(8,128)S(1)}) custom-call(f32[16,2,8,128]{3,2,1,0:T(8,128)S(1)} %collective-permute-done.5.r1p, f32[16,2,8,128]{3,2,1,0:T(8,128)S(1)} %get-tuple-element.45.r1, f32[16,2,8,128]{3,2,1,0:T(8,128)S(1)} %collective-permute-done.6.r1n, ...), custom_call_target="tpu_custom_call" | custom-call | flops 6225920 | bytes 1556480 | tf_op jit(solution)/shard_map/middle_first/pallas_call | solution.py:545
  37.1 12.6 %all_to_all.22 = f32[32,4,128]{2,1,0:T(4,128)S(1)} all-to-all(f32[32,4,128]{2,1,0:T(4,128)S(1)} %bitcast.10), channel_id=1, replica_groups=mesh['die'=4,'tile'=8] {'die','tile'}, dimensions={0} | all-to-all | bytes 131072 | tf_op jit(solution)/shard_map/all_to_all | solution.py:612
  49.8 0.0 copy-done
  49.8 0.0 copy-done.3
  49.8 7.8 %back.1 = (f32[18,5,32,128]{3,2,1,0:T(8,128)S(1)}, f32[16,2,8,128]{3,2,1,0:T(8,128)S(1)}) custom-call(f32[128,128]{1,0:T(8,128)S(1)} %bitcast.8, f32[16,8,128]{2,1,0:T(8,128)S(1)} %get-tuple-element.49.u2, f32[16,8,128]{2,1,0:T(8,128)S(1)} %get-tuple-element.50.l2, f32[16,8,128]{2,1,0:T(8,128)S(1)} %get-tuple-element.51.d2, ...), custom_call_target="tpu_custom_call" | custom-call | flops 35454976 | bytes 8863744 | tf_op jit(solution)/shard_map/back/pallas_call | solution.py:545
  57.6 0.4 collective-permute-start.8
  58.0 1.4 %collective-permute-start.7 = (f32[16,2,8,128]{3,2,1,0:T(8,128)S(1)}, f32[16,2,8,128]{3,2,1,0:T(8,128)S(1)}, u32[]{:S(2)}, u32[]{:S(2)}) collective-permute-start(f32[16,2,8,128]{3,2,1,0:T(8,128)S(1)} %get-tuple-element.57.r1), channel_id=1, source_target_pairs={{0,1},{1,2},{2,3},{3,4},{4,5},{5,6},{6,7},{7,0},{8,9},{9,10},{10,1... | collective-permute-start | bytes 393224 | tf_op jit(solution)/shard_map/ppermute | solution.py:561
  59.4 2.6 %collective-permute-done.8.r1n = f32[16,2,8,128]{3,2,1,0:T(8,128)S(1)} collective-permute-done((f32[16,2,8,128]{3,2,1,0:T(8,128)S(1)}, f32[16,2,8,128]{3,2,1,0:T(8,128)S(1)}, u32[]{:S(2)}, u32[]{:S(2)}) %collective-permute-start.8) | collective-permute-done | bytes 131104 | tf_op jit(solution)/shard_map/ppermute | solution.py:561
  62.0 0.0 collective-permute-done.7.r1p
  62.0 1.1 %middle_first.3 = (f32[16,2,16,128]{3,2,1,0:T(8,128)S(1)}, f32[18,2,16,128]{3,2,1,0:T(8,128)S(1)}, f32[128,128]{1,0:T(8,128)S(1)}) custom-call(f32[16,2,8,128]{3,2,1,0:T(8,128)S(1)} %collective-permute-done.7.r1p, f32[16,2,8,128]{3,2,1,0:T(8,128)S(1)} %get-tuple-element.57.r1, f32[16,2,8,128]{3,2,1,0:T(8,128)S(1)} %collective-permute-done.8.r1n, ...), custom_call_target="tpu_custom_call" | custom-call | flops 6225920 | bytes 1556480 | tf_op jit(solution)/shard_map/middle_first/pallas_call | solution.py:545
  63.1 11.4 %all_to_all.23 = f32[32,4,128]{2,1,0:T(4,128)S(1)} all-to-all(f32[32,4,128]{2,1,0:T(4,128)S(1)} %bitcast.9), channel_id=1, replica_groups=mesh['die'=4,'tile'=8] {'die','tile'}, dimensions={0} | all-to-all | bytes 131072 | tf_op jit(solution)/shard_map/all_to_all | solution.py:612
  74.5 5.1 %last.1 = (f32[2,4,16,512]{3,2,1,0:T(8,128)S(1)}, f32[2,4,16,512]{3,2,1,0:T(8,128)S(1)}, f32[2,4,16,512]{3,2,1,0:T(8,128)S(1)}, f32[2,4,16,512]{3,2,1,0:T(8,128)S(1)}) custom-call(f32[128,128]{1,0:T(8,128)S(1)} %bitcast.7, f32[16,8,128]{2,1,0:T(8,128)S(1)} %get-tuple-element.49.u2, f32[16,8,128]{2,1,0:T(8,128)S(1)} %get-tuple-element.50.l2, ...), custom_call_target="tpu_custom_call" | custom-call | flops 30605312 | bytes 7651328 | tf_op jit(solution)/shard_map/last/pallas_call | solution.py:545
  79.5 0.1 collective-permute-start.9
  79.6 0.6 collective-permute-start.10
  80.2 2.0 %collective-permute-start.11 = (f32[2,4,16,512]{3,2,1,0:T(8,128)S(1)}, f32[2,4,16,512]{3,2,1,0:T(8,128)S(1)}, u32[]{:S(2)}, u32[]{:S(2)}) collective-permute-start(f32[2,4,16,512]{3,2,1,0:T(8,128)S(1)} %get-tuple-element.65), channel_id=1, source_target_pairs={{0,24},{8,0},{16,8},{24,16},{1,25},{9,1},{17,9},{25,17},{2,26},{10... | collective-permute-start | bytes 786440 | tf_op jit(solution)/shard_map/ppermute | solution.py:561
  82.2 5.8 %collective-permute-done.9.refs_1_ = f32[2,4,16,512]{3,2,1,0:T(8,128)S(1)} collective-permute-done((f32[2,4,16,512]{3,2,1,0:T(8,128)S(1)}, f32[2,4,16,512]{3,2,1,0:T(8,128)S(1)}, u32[]{:S(2)}, u32[]{:S(2)}) %collective-permute-start.9) | collective-permute-done | bytes 262176 | tf_op jit(solution)/shard_map/ppermute | solution.py:561
  88.0 4.7 %collective-permute-done.10.refs_2_ = f32[2,4,16,512]{3,2,1,0:T(8,128)S(1)} collective-permute-done((f32[2,4,16,512]{3,2,1,0:T(8,128)S(1)}, f32[2,4,16,512]{3,2,1,0:T(8,128)S(1)}, u32[]{:S(2)}, u32[]{:S(2)}) %collective-permute-start.10) | collective-permute-done | bytes 262176 | tf_op jit(solution)/shard_map/ppermute | solution.py:561
  92.7 0.0 collective-permute-done.11.refs_3_
  92.7 1.0 %unpack.1 = (f32[4,16,2048]{2,1,0:T(8,128)}, f32[4,16,2048]{2,1,0:T(8,128)}) custom-call(f32[2,4,16,512]{3,2,1,0:T(8,128)S(1)} %get-tuple-element.62.refs_0_, f32[2,4,16,512]{3,2,1,0:T(8,128)S(1)} %collective-permute-done.9.refs_1_, f32[2,4,16,512]{3,2,1,0:T(8,128)S(1)} %collective-permute-done.10.refs_2_, f32[2,4,16,512]{3,2,1,0:T(8,128)S(1)} %collective-permute-done.11.refs_3_), custom_call_target="tpu_custom_call" | custom-call | flops 8388608 | bytes 2097152 | tf_op jit(solution)/shard_map/unpack/pallas_call | solution.py:545
Async XLA Ops:
  0.6 27.9 %copy-start.1 = (bf16[640,256]{1,0:T(8,128)(2,1)S(1)}, bf16[640,256]{1,0:T(8,128)(2,1)}, u32[]{:S(2)}) copy-start(bf16[640,256]{1,0:T(8,128)(2,1)} %constant.8.clone.down) | copy-start | bytes 983044
  1.3 1.0 %copy-start.2 = (f32[4,16,2048]{2,1,0:T(8,128)S(1)}, f32[4,16,2048]{2,1,0:T(8,128)}, u32[]{:S(2)}) copy-start(f32[4,16,2048]{2,1,0:T(8,128)} %f_h.1) | copy-start | bytes 1572868
  2.4 0.7 copy-start.5
  3.1 0.7 copy-start.6
  3.7 0.7 copy-start.7
  5.1 7.1 %collective-permute-start = (f32[328,128]{1,0:T(8,128)S(1)}, f32[328,128]{1,0:T(8,128)S(1)}, u32[]{:S(2)}, u32[]{:S(2)}) collective-permute-start(f32[328,128]{1,0:T(8,128)S(1)} %get-tuple-element.35), channel_id=1, source_target_pairs={{0,8},{8,16},{16,24},{24,0},{1,9},{9,17},{17,25},{25,1},{2,10},{10... | collective-permute-start | bytes 503816 | tf_op jit(solution)/shard_map/ppermute | solution.py:561
  7.2 9.3 %collective-permute-start.1 = (f32[328,128]{1,0:T(8,128)S(1)}, f32[328,128]{1,0:T(8,128)S(1)}, u32[]{:S(2)}, u32[]{:S(2)}) collective-permute-start(f32[328,128]{1,0:T(8,128)S(1)} %get-tuple-element.36), channel_id=1, source_target_pairs={{0,16},{8,24},{16,0},{24,8},{1,17},{9,25},{17,1},{25,9},{2,18},{10... | collective-permute-start | bytes 503816 | tf_op jit(solution)/shard_map/ppermute | solution.py:561
  8.5 8.1 %collective-permute-start.2 = (f32[328,128]{1,0:T(8,128)S(1)}, f32[328,128]{1,0:T(8,128)S(1)}, u32[]{:S(2)}, u32[]{:S(2)}) collective-permute-start(f32[328,128]{1,0:T(8,128)S(1)} %get-tuple-element.37), channel_id=1, source_target_pairs={{0,24},{8,0},{16,8},{24,16},{1,25},{9,1},{17,9},{25,17},{2,26},{10... | collective-permute-start | bytes 503816 | tf_op jit(solution)/shard_map/ppermute | solution.py:561
  16.6 7.0 %collective-permute-start.3 = (f32[80,8,128]{2,1,0:T(8,128)S(1)}, f32[80,8,128]{2,1,0:T(8,128)S(1)}, u32[]{:S(2)}, u32[]{:S(2)}) collective-permute-start(f32[80,8,128]{2,1,0:T(8,128)S(1)} %get-tuple-element.38.bot), channel_id=1, source_target_pairs={{0,1},{1,2},{2,3},{3,4},{4,5},{5,6},{6,7},{7,0},{8,9},{9,10},{10,1... | collective-permute-start | bytes 983048 | tf_op jit(solution)/shard_map/ppermute | solution.py:561
  18.6 9.9 %collective-permute-start.4 = (f32[80,8,128]{2,1,0:T(8,128)S(1)}, f32[80,8,128]{2,1,0:T(8,128)S(1)}, u32[]{:S(2)}, u32[]{:S(2)}) collective-permute-start(f32[80,8,128]{2,1,0:T(8,128)S(1)} %get-tuple-element.39.top), channel_id=1, source_target_pairs={{0,7},{1,0},{2,1},{3,2},{4,3},{5,4},{6,5},{7,6},{8,15},{9,8},{10,9... | collective-permute-start | bytes 983048 | tf_op jit(solution)/shard_map/ppermute | solution.py:561
  28.5 7.5 %copy-start.4 = (bf16[128,128]{1,0:T(8,128)(2,1)S(1)}, bf16[128,128]{1,0:T(8,128)(2,1)}, u32[]{:S(2)}) copy-start(bf16[128,128]{1,0:T(8,128)(2,1)} %constant.11.clone.down2) | copy-start | bytes 98308
  28.6 21.2 %copy-start = (bf16[256,640]{1,0:T(8,128)(2,1)S(1)}, bf16[256,640]{1,0:T(8,128)(2,1)}, u32[]{:S(2)}) copy-start(bf16[256,640]{1,0:T(8,128)(2,1)} %constant.9.clone.spread1) | copy-start | bytes 983044
  28.6 21.2 %copy-start.3 = (bf16[128,256]{1,0:T(8,128)(2,1)S(1)}, bf16[128,256]{1,0:T(8,128)(2,1)}, u32[]{:S(2)}) copy-start(bf16[128,256]{1,0:T(8,128)(2,1)} %constant.10.clone.spread2) | copy-start | bytes 196612
  31.2 4.4 %collective-permute-start.6 = (f32[16,2,8,128]{3,2,1,0:T(8,128)S(1)}, f32[16,2,8,128]{3,2,1,0:T(8,128)S(1)}, u32[]{:S(2)}, u32[]{:S(2)}) collective-permute-start(f32[16,2,8,128]{3,2,1,0:T(8,128)S(1)} %get-tuple-element.45.r1), channel_id=1, source_target_pairs={{0,7},{1,0},{2,1},{3,2},{4,3},{5,4},{6,5},{7,6},{8,15},{9,8},{10,9... | collective-permute-start | bytes 393224 | tf_op jit(solution)/shard_map/ppermute | solution.py:561
  31.2 4.8 %collective-permute-start.5 = (f32[16,2,8,128]{3,2,1,0:T(8,128)S(1)}, f32[16,2,8,128]{3,2,1,0:T(8,128)S(1)}, u32[]{:S(2)}, u32[]{:S(2)}) collective-permute-start(f32[16,2,8,128]{3,2,1,0:T(8,128)S(1)} %get-tuple-element.45.r1), channel_id=1, source_target_pairs={{0,1},{1,2},{2,3},{3,4},{4,5},{5,6},{6,7},{7,0},{8,9},{9,10},{10,1... | collective-permute-start | bytes 393224 | tf_op jit(solution)/shard_map/ppermute | solution.py:561
  57.6 4.4 %collective-permute-start.8 = (f32[16,2,8,128]{3,2,1,0:T(8,128)S(1)}, f32[16,2,8,128]{3,2,1,0:T(8,128)S(1)}, u32[]{:S(2)}, u32[]{:S(2)}) collective-permute-start(f32[16,2,8,128]{3,2,1,0:T(8,128)S(1)} %get-tuple-element.57.r1), channel_id=1, source_target_pairs={{0,7},{1,0},{2,1},{3,2},{4,3},{5,4},{6,5},{7,6},{8,15},{9,8},{10,9... | collective-permute-start | bytes 393224 | tf_op jit(solution)/shard_map/ppermute | solution.py:561
  58.0 4.0 %collective-permute-start.7 = (f32[16,2,8,128]{3,2,1,0:T(8,128)S(1)}, f32[16,2,8,128]{3,2,1,0:T(8,128)S(1)}, u32[]{:S(2)}, u32[]{:S(2)}) collective-permute-start(f32[16,2,8,128]{3,2,1,0:T(8,128)S(1)} %get-tuple-element.57.r1), channel_id=1, source_target_pairs={{0,1},{1,2},{2,3},{3,4},{4,5},{5,6},{6,7},{7,0},{8,9},{9,10},{10,1... | collective-permute-start | bytes 393224 | tf_op jit(solution)/shard_map/ppermute | solution.py:561
  79.5 8.5 %collective-permute-start.9 = (f32[2,4,16,512]{3,2,1,0:T(8,128)S(1)}, f32[2,4,16,512]{3,2,1,0:T(8,128)S(1)}, u32[]{:S(2)}, u32[]{:S(2)}) collective-permute-start(f32[2,4,16,512]{3,2,1,0:T(8,128)S(1)} %get-tuple-element.63), channel_id=1, source_target_pairs={{0,8},{8,16},{16,24},{24,0},{1,9},{9,17},{17,25},{25,1},{2,10},{10... | collective-permute-start | bytes 786440 | tf_op jit(solution)/shard_map/ppermute | solution.py:561
  79.6 13.1 %collective-permute-start.10 = (f32[2,4,16,512]{3,2,1,0:T(8,128)S(1)}, f32[2,4,16,512]{3,2,1,0:T(8,128)S(1)}, u32[]{:S(2)}, u32[]{:S(2)}) collective-permute-start(f32[2,4,16,512]{3,2,1,0:T(8,128)S(1)} %get-tuple-element.64), channel_id=1, source_target_pairs={{0,16},{8,24},{16,0},{24,8},{1,17},{9,25},{17,1},{25,9},{2,18},{10... | collective-permute-start | bytes 786440 | tf_op jit(solution)/shard_map/ppermute | solution.py:561
  80.2 12.5 %collective-permute-start.11 = (f32[2,4,16,512]{3,2,1,0:T(8,128)S(1)}, f32[2,4,16,512]{3,2,1,0:T(8,128)S(1)}, u32[]{:S(2)}, u32[]{:S(2)}) collective-permute-start(f32[2,4,16,512]{3,2,1,0:T(8,128)S(1)} %get-tuple-element.65), channel_id=1, source_target_pairs={{0,24},{8,0},{16,8},{24,16},{1,25},{9,1},{17,9},{25,17},{2,26},{10... | collective-permute-start | bytes 786440 | tf_op jit(solution)/shard_map/ppermute | solution.py:561
